TPU v7x, 32 devices: a whole 2x2x4 slice. The times are simulated.
32 devices in a mesh: clip: 8 (over z, x), freq: 4 (over y, core).
Axes of the slice: x: 2, y: 2, z: 4, core: 2. Of those that a mesh axis runs over, the one named last changes fastest.
Arguments:
- tokens: bfloat16 [24, 1192, 768], P('clip', 'freq'), may hold values from -6 to 6
- kept_counts: int32 [24, 4], P('clip', 'freq'), may hold values from 37 to 298, as said below
- attn_gain: bfloat16 [768], replicated, may hold values from 0.099609375 to 1.8984375
- attn_shift: bfloat16 [768], replicated, may hold values from -3 to 3
- qkv_weight: bfloat16 [768, 2304], replicated, may hold values from -0.3125 to 0.3125
- query_bias: bfloat16 [768], replicated, may hold values from -3 to 3
- value_bias: bfloat16 [768], replicated, may hold values from -3 to 3
- proj_weight: bfloat16 [768, 768], replicated, may hold values from -1.75 to 1.75
- proj_bias: bfloat16 [768], replicated, may hold values from -3 to 3
- mlp_gain: bfloat16 [768], replicated, may hold values from 0.099609375 to 1.8984375
- mlp_shift: bfloat16 [768], replicated, may hold values from -3 to 3
- fc1_weight: bfloat16 [768, 3072], replicated, may hold values from -0.21875 to 0.21875
- fc1_bias: bfloat16 [3072], replicated, may hold values from -3 to 3
- fc2_weight: bfloat16 [3072, 768], replicated, may hold values from -0.15625 to 0.15625
- fc2_bias: bfloat16 [768], replicated, may hold values from -3 to 3
- cotangent: bfloat16 [24, 1192, 768], P('clip', 'freq'), may hold values from -6 to 6
Outputs:
- layer_out: bfloat16 [24, 1192, 768], P('clip', 'freq')
- grad_tokens: float32 [24, 1192, 768], P('clip', 'freq')
- grad_attn_gain: float32 [768], replicated
- grad_attn_shift: float32 [768], replicated
- grad_qkv_weight: float32 [768, 2304], P('clip')
- grad_query_bias: float32 [768], replicated
- grad_value_bias: float32 [768], replicated
- grad_proj_weight: float32 [768, 768], P('clip')
- grad_proj_bias: float32 [768], replicated
- grad_mlp_gain: float32 [768], replicated
- grad_mlp_shift: float32 [768], replicated
- grad_fc1_weight: float32 [768, 3072], P('clip')
- grad_fc1_bias: float32 [3072], replicated
- grad_fc2_weight: float32 [3072, 768], P('clip')
- grad_fc2_bias: float32 [768], replicated
Inputs may be any that keep to these rules, and one draw needn't show every extreme that they name: `kept_counts`: each clip keeps all 298 slots in every group, or between 37 and 149 in each group; clip 0 keeps all; kept tokens fill the first slots of a group.
All inputs are finite; a program needn't handle non-finite values.
Results may differ from a plain program's by a relative error of at most 0.015.
The roundings to bfloat16 on the way count: a program that leaves them out, or rounds other values in their place, can miss the bound.
Values may be sent and summed in bfloat16 or wider, within the bound.
A program may use at most 320 MiB of HBM per device.

v0:
```python
import functools
import math

import jax
import jax.numpy as jnp
from jax import lax
from jax.experimental import pallas as pl
from jax.experimental.pallas import tpu as pltpu
from jax.sharding import PartitionSpec as P

HEADS = 12
DH = 64
EPS = 1e-06
MASKED = -1000000000.0
VMEM_BYTES = 60 * 1024 * 1024

f32 = jnp.float32
bf16 = jnp.bfloat16
NN = (((1,), (0,)), ((), ()))
NT = (((1,), (1,)), ((), ()))
TN = (((0,), (0,)), ((), ()))


def dot(left, right, dims=NN):
    return lax.dot_general(left, right, dims, preferred_element_type=f32)


def center_scale(rows):
    center = rows - jnp.mean(rows, axis=-1, keepdims=True)
    inverse = lax.rsqrt(jnp.mean(center * center, axis=-1, keepdims=True) + EPS)
    return center * inverse, inverse


def norm_back(unit, inverse, gain, grad):
    scaled = grad * gain
    return inverse * (
        scaled
        - jnp.mean(scaled, axis=-1, keepdims=True)
        - unit * jnp.mean(scaled * unit, axis=-1, keepdims=True)
    )


def column_sums(rows):
    return jnp.sum(rows, axis=0, keepdims=True)


def own_lanes(shape, head):
    lane = lax.broadcasted_iota(jnp.int32, shape, len(shape) - 1)
    return lane < DH if head == 0 else lane >= DH


def only(rows, head):
    return jnp.where(own_lanes(rows.shape, head), rows, jnp.zeros_like(rows))


def full(shape):
    return pl.BlockSpec(shape, lambda *ids: (0,) * len(shape))


def params(**more):
    return pltpu.CompilerParams(vmem_limit_bytes=VMEM_BYTES, **more)


def partner(kind):
    index = lax.axis_index("freq")
    if kind == "vert":
        return {"freq": (index + 2) % 4}
    return {"freq": index + 1 - 2 * (index % 2)}


def forward_kernel(
    counts,
    tok_ref, qkv_ref, qb_ref, vb_ref, gain_ref, shift_ref, proj_ref, pb_ref, gain2_ref, shift2_ref,
    q_ref, k_ref, v_ref, normed_ref, mixed_ref, lse_ref, middle_ref, normed2_ref, mask_ref,
    held, send_sem, recv_sem,
):
    clips, slots, rows = counts
    clip = pl.program_id(0)
    pair = pl.program_id(1)
    width = tok_ref.shape[-1]

    def copy(kind, index):
        at = {"vert": 0, "core": 1, "diag": 2}[kind]
        return pltpu.make_async_remote_copy(
            src_ref=held.at[index, 0] if kind == "diag" else tok_ref.at[index],
            dst_ref=held.at[index, at],
            send_sem=send_sem.at[index, at],
            recv_sem=recv_sem.at[index, at],
            device_id=partner(kind),
            device_id_type=pl.DeviceIdType.MESH,
        )

    def project(slot, source):
        unit, _ = center_scale(source.astype(f32))
        normed = (unit * gain_ref[...] + shift_ref[...]).astype(bf16)
        if slot == 0:
            normed_ref[0] = normed
            query = (dot(normed, qkv_ref[:, :width]) + qb_ref[...]).astype(bf16)
            q_ref[0] = query * jnp.asarray(DH ** -0.5, bf16)
        both = dot(normed, qkv_ref[:, width:])
        k_ref[0, slot * rows : (slot + 1) * rows] = both[:, :width].astype(bf16)
        v_ref[0, slot * rows : (slot + 1) * rows] = (both[:, width:] + vb_ref[...]).astype(bf16)
        first = (slots // 16) * 16
        kept = source[first:].astype(f32)[slots - first : slots - first + 1, 0:1] + slots // 2
        lane = lax.broadcasted_iota(jnp.int32, (1, rows), 1).astype(f32)
        return (lane < kept).astype(f32)

    @pl.when((clip == 0) & (pair == 0))
    def enter():
        barrier = pltpu.get_barrier_semaphore()
        for kind in ("vert", "core"):
            pl.semaphore_signal(
                barrier, inc=1, device_id=partner(kind), device_id_type=pl.DeviceIdType.MESH
            )
        pl.semaphore_wait(barrier, 2)
        copy("vert", 0).start()
        for index in range(clips):
            copy("core", index).start()

    def pass_on(index):
        copy("vert", index).wait_recv()
        copy("diag", index).start()
        copy("vert", index).wait_send()

        @pl.when(index + 1 < clips)
        def more():
            copy("vert", index + 1).start()

    @pl.when(pair == 0)
    def project_all():
        live_own = project(0, tok_ref[clip])
        copy("core", clip).wait_recv()
        live_core = project(2, held[clip, 1])

        @pl.when(clip == 0)
        def first_pass():
            pass_on(clip)

        live_vert = project(1, held[clip, 0])
        copy("diag", clip).wait_recv()
        live_diag = project(3, held[clip, 2])
        mask_ref[0] = jnp.concatenate([live_own, live_vert, live_core, live_diag], axis=1)

    @pl.when((pair == 3) & (clip + 1 < clips))
    def next_pass():
        pass_on(clip + 1)

    lanes = pl.ds(pl.multiple_of(pair * 2 * DH, 2 * DH), 2 * DH)
    query = q_ref[0, :, lanes]
    keys = k_ref[0, :, lanes]
    values = v_ref[0, :, lanes]
    live = mask_ref[0] > 0.5
    outs, lses = [], []
    for head in range(2):
        scores = jnp.where(live, dot(only(query, head), keys, NT), MASKED)
        top = jnp.max(scores, axis=1, keepdims=True)
        exps = jnp.exp(scores - top)
        total = jnp.sum(exps, axis=1, keepdims=True)
        outs.append(dot(exps.astype(bf16), values) / total)
        lses.append(top + jnp.log(total))
    first = own_lanes(outs[0].shape, 0)
    mixed_ref[0, :, lanes] = jnp.where(first, outs[0], outs[1]).astype(bf16)
    lse_ref[0, :, lanes] = jnp.where(first, lses[0], lses[1])

    @pl.when(pair == pl.num_programs(1) - 1)
    def finish():
        middle = tok_ref[clip].astype(f32) + (dot(mixed_ref[0], proj_ref[...]) + pb_ref[...])
        middle_ref[0] = middle
        unit, _ = center_scale(middle)
        normed2_ref[0] = (unit * gain2_ref[...] + shift2_ref[...]).astype(bf16)
        copy("core", clip).wait_send()
        copy("diag", clip).wait_send()


def forward(tok, slots, qkv_weight, vectors, proj_weight):
    clips, rows, width = tok.shape
    keys = 4 * rows
    pairs = HEADS // 2
    query_bias, value_bias, gain, shift, proj_bias, gain2, shift2 = vectors
    one = pl.Buffered(buffer_count=1)
    row = full((1, width))
    block = lambda n: pl.BlockSpec((1, n, width), lambda c, p: (c, 0, 0))
    flops = 2 * clips * (10 * rows * width * width + 2 * rows * keys * width)
    weight = lambda w: pl.BlockSpec(w.shape, lambda c, p: (0, 0), pipeline_mode=one)
    return pl.pallas_call(
        functools.partial(forward_kernel, (clips, slots, rows)),
        grid=(clips, pairs),
        in_specs=[
            pl.BlockSpec(tok.shape, lambda c, p: (0, 0, 0), pipeline_mode=one),
            weight(qkv_weight), row, row, row, row, weight(proj_weight), row, row, row,
        ],
        out_specs=[block(rows), block(keys), block(keys)] + [block(rows)] * 5
        + [pl.BlockSpec((1, 1, keys), lambda c, p: (c, 0, 0))],
        out_shape=[
            jax.ShapeDtypeStruct((clips, rows, width), bf16),
            jax.ShapeDtypeStruct((clips, keys, width), bf16),
            jax.ShapeDtypeStruct((clips, keys, width), bf16),
            jax.ShapeDtypeStruct((clips, rows, width), bf16),
            jax.ShapeDtypeStruct((clips, rows, width), bf16),
            jax.ShapeDtypeStruct((clips, rows, width), f32),
            jax.ShapeDtypeStruct((clips, rows, width), f32),
            jax.ShapeDtypeStruct((clips, rows, width), bf16),
            jax.ShapeDtypeStruct((clips, 1, keys), f32),
        ],
        scratch_shapes=[
            pltpu.VMEM((clips, 3, rows, width), bf16),
            pltpu.SemaphoreType.DMA((clips, 3)),
            pltpu.SemaphoreType.DMA((clips, 3)),
        ],
        compiler_params=params(collective_id=0, has_side_effects=True),
        cost_estimate=pl.CostEstimate(
            flops=flops, bytes_accessed=40_000_000, transcendentals=clips * rows * keys * HEADS
        ),
        name="forward",
    )(tok, qkv_weight, query_bias, value_bias, gain, shift, proj_weight, proj_bias, gain2, shift2)


def mlp_kernel(
    counts,
    n2_ref, middle_ref, cot_ref, live_ref, mixed_ref, fc1_ref, b1_ref, fc2_ref, b2_ref,
    gain_ref, shift_ref, proj_ref,
    out_ref, dfc1_ref, dfc2_ref, dproj_ref, db1_ref, small_ref, gmid_ref, gmixed_ref,
    n2t_ref, grad_ref, out_acc, dn_acc, hidden_ref, dact_ref, active_ref, dhid_ref,
):
    clips, slots, rows, tile = counts
    step = pl.program_id(0)
    width = n2_ref.shape[-1]
    chunk = fc1_ref.shape[-1]
    total = clips * rows

    @pl.when(step == 0)
    def start():
        n2t_ref[...] = n2_ref[...].T
        grad_ref[...] = (cot_ref[...].astype(f32) * live_ref[...]).astype(bf16)
        out_acc[...] = jnp.zeros_like(out_acc)
        dn_acc[...] = jnp.zeros_like(dn_acc)

    hidden_ref[...] = dot(n2_ref[...], fc1_ref[...])
    dact_ref[...] = dot(grad_ref[...], fc2_ref[...], NT)
    bias = b1_ref[...]

    def gelu_tile(index, sums):
        at = pl.ds(pl.multiple_of(index * tile, tile), tile)
        hidden = hidden_ref[at, :] + bias
        cdf = 0.5 * (1.0 + lax.erf(hidden * (0.5 ** 0.5)))
        active_ref[at, :] = (hidden * cdf).astype(bf16)
        slope = cdf + hidden * (jnp.exp(-0.5 * hidden * hidden) * (1.0 / math.sqrt(2.0 * math.pi)))
        dhid = (dact_ref[at, :] * slope).astype(bf16)
        dhid_ref[at, :] = dhid
        return sums + dhid.astype(f32)

    sums = lax.fori_loop(0, total // tile, gelu_tile, jnp.zeros((tile, chunk), f32))
    db1_ref[...] = column_sums(sums)
    active = active_ref[...]
    dhid = dhid_ref[...]
    out_acc[...] += dot(active, fc2_ref[...])
    dn_acc[...] += dot(dhid, fc1_ref[...], NT)
    dfc1_ref[0] = dot(n2t_ref[...], dhid).astype(bf16)
    dfc2 = dot(active, grad_ref[...], TN).astype(bf16)
    half = width // 2
    dfc2_ref[0] = dfc2[:, :half]
    dfc2_ref[1] = dfc2[:, half:]

    @pl.when(step == pl.num_programs(0) - 1)
    def finish():
        gain = gain_ref[...]
        sum_gain = jnp.zeros((1, width), f32)
        sum_shift = jnp.zeros((1, width), f32)
        sum_grad = jnp.zeros((1, width), f32)
        sum_proj = jnp.zeros((1, width), f32)
        for clip in range(clips):
            at = slice(clip * rows, (clip + 1) * rows)
            middle = middle_ref[at]
            live = live_ref[at]
            layer = live * (middle + (out_acc[at] + b2_ref[...]))
            out_ref[clip] = layer[:slots].astype(bf16)
            unit, inverse = center_scale(middle)
            grad = dn_acc[at]
            out_grad = cot_ref[at].astype(f32) * live
            gmid = out_grad + norm_back(unit, inverse, gain, grad)
            gmid_ref[at] = gmid
            low = gmid.astype(bf16)
            dhid_ref[at, :width] = low
            gmixed_ref[at] = dot(low, proj_ref[...], NT).astype(bf16)
            sum_gain += column_sums(grad * unit)
            sum_shift += column_sums(grad)
            sum_grad += column_sums(grad_ref[at].astype(f32))
            sum_proj += column_sums(low.astype(f32))
        dproj = dot(mixed_ref[...], dhid_ref[:, :width], TN).astype(bf16)
        dproj_ref[0] = dproj[:, :half]
        dproj_ref[1] = dproj[:, half:]
        small_ref[0:1] = sum_gain
        small_ref[1:2] = sum_shift
        small_ref[2:3] = sum_grad
        small_ref[3:4] = sum_proj


def mlp(n2, middle, cot, live, mixed, fc1, b1, fc2, b2, gain, shift, proj, shape):
    clips, slots, rows = shape
    total, width = n2.shape
    hidden = fc1.shape[1]
    chunk = 768
    steps = hidden // chunk
    half = steps // 2
    tile = 16
    row = full((1, width))
    one = pl.Buffered(buffer_count=1)
    big = pl.BlockSpec((total, width), lambda j: (0, 0), pipeline_mode=one)
    return pl.pallas_call(
        functools.partial(mlp_kernel, (clips, slots, rows, tile)),
        grid=(steps,),
        in_specs=[
            big, big, big,
            pl.BlockSpec((total, 1), lambda j: (0, 0), pipeline_mode=one),
            big,
            pl.BlockSpec((width, chunk), lambda j: (0, j)),
            pl.BlockSpec((1, chunk), lambda j: (0, j)),
            pl.BlockSpec((chunk, width), lambda j: (j, 0)),
            row, row, row,
            pl.BlockSpec((width, width), lambda j: (0, 0), pipeline_mode=one),
        ],
        out_specs=[
            full((clips, slots, width)),
            pl.BlockSpec((1, width, chunk), lambda j: (j // half, 0, j % half)),
            pl.BlockSpec((2, chunk, width // 2), lambda j: (0, j, 0)),
            full((2, width, width // 2)),
            pl.BlockSpec((1, chunk), lambda j: (0, j)),
            full((8, width)),
            full((total, width)),
            full((total, width)),
        ],
        out_shape=[
            jax.ShapeDtypeStruct((clips, slots, width), bf16),
            jax.ShapeDtypeStruct((2, width, hidden // 2), bf16),
            jax.ShapeDtypeStruct((2, hidden, width // 2), bf16),
            jax.ShapeDtypeStruct((2, width, width // 2), bf16),
            jax.ShapeDtypeStruct((1, hidden), f32),
            jax.ShapeDtypeStruct((8, width), f32),
            jax.ShapeDtypeStruct((total, width), f32),
            jax.ShapeDtypeStruct((total, width), bf16),
        ],
        scratch_shapes=[
            pltpu.VMEM((width, total), bf16),
            pltpu.VMEM((total, width), bf16),
            pltpu.VMEM((total, width), f32),
            pltpu.VMEM((total, width), f32),
            pltpu.VMEM((total, chunk), f32),
            pltpu.VMEM((total, chunk), f32),
            pltpu.VMEM((total, chunk), bf16),
            pltpu.VMEM((total, chunk), bf16),
        ],
        compiler_params=params(),
        cost_estimate=pl.CostEstimate(
            flops=12 * total * width * hidden, bytes_accessed=40_000_000, transcendentals=2 * total * hidden
        ),
        name="mlp",
    )(n2, middle, cot, live, mixed, fc1, b1, fc2, b2, gain, shift, proj)


def attend_back_kernel(q_ref, k_ref, v_ref, mask_ref, mixed_ref, lse_ref, grad_ref,
                       dq_ref, dkeep_ref, dsend_ref):
    query = q_ref[0]
    keys = k_ref[0]
    values = v_ref[0]
    grad = grad_ref[0]
    live = mask_ref[0] > 0.5
    product = grad.astype(f32) * mixed_ref[0].astype(f32)
    dqs, dk, dv = [], None, None
    for head in range(2):
        own_query = only(query, head)
        own_grad = only(grad, head)
        scores = jnp.where(live, dot(own_query, keys, NT), MASKED)
        probs = jnp.exp(scores - lse_ref[0, :, head * DH : head * DH + 1])
        delta = jnp.sum(only(product, head), axis=1, keepdims=True)
        dscores = (probs * (dot(own_grad, values, NT) - delta)).astype(bf16)
        dqs.append(dot(dscores, keys))
        more_k = dot(dscores, own_query, TN)
        more_v = dot(probs.astype(bf16), own_grad, TN)
        dk = more_k if dk is None else dk + more_k
        dv = more_v if dv is None else dv + more_v
    first = own_lanes(dqs[0].shape, 0)
    dq_ref[0] = (jnp.where(first, dqs[0], dqs[1]) * DH ** -0.5).astype(bf16)
    half = dk.shape[0] // 2
    dkeep_ref[0, 0] = dk[:half].astype(bf16)
    dkeep_ref[1, 0] = dv[:half].astype(bf16)
    dsend_ref[0, 0] = dk[half:].astype(bf16)
    dsend_ref[1, 0] = dv[half:].astype(bf16)


def attend_back(q, k, v, mask, mixed, lse, grad, first_pair, pairs):
    clips, rows, _ = q.shape
    keys = k.shape[1]
    lanes = 2 * DH
    tok = pl.BlockSpec((1, rows, lanes), lambda c, p: (c, 0, first_pair + p))
    key = pl.BlockSpec((1, keys, lanes), lambda c, p: (c, 0, first_pair + p))
    part = pl.BlockSpec((2, 1, keys // 2, lanes), lambda c, p: (0, c, 0, p))
    return pl.pallas_call(
        attend_back_kernel,
        grid=(clips, pairs),
        in_specs=[tok, key, key, pl.BlockSpec((1, 1, keys), lambda c, p: (c, 0, 0)), tok, tok, tok],
        out_specs=[pl.BlockSpec((1, rows, lanes), lambda c, p: (c, 0, p)), part, part],
        out_shape=[
            jax.ShapeDtypeStruct((clips, rows, pairs * lanes), bf16),
            jax.ShapeDtypeStruct((2, clips, keys // 2, pairs * lanes), bf16),
            jax.ShapeDtypeStruct((2, clips, keys // 2, pairs * lanes), bf16),
        ],
        compiler_params=params(),
        cost_estimate=pl.CostEstimate(
            flops=4 * 10 * clips * rows * keys * pairs * lanes,
            bytes_accessed=clips * pairs * lanes * (keys * 10 + rows * 12),
            transcendentals=clips * rows * keys * 2 * pairs,
        ),
        name="attend_back",
    )(q, k, v, mask, mixed, lse, grad)


def weight_kernel(normed_ref, dq_ref, dk0_ref, dk1_ref, dk2_ref, out_ref, dkv_ref, sums_ref):
    part = pl.program_id(0)
    @pl.when(part == 0)
    def query():
        grad = dq_ref[...]
        out_ref[0] = dot(normed_ref[...], grad, TN).astype(bf16)
        sums_ref[0] = column_sums(grad.astype(f32))
        dkv_ref[0] = jnp.zeros_like(dkv_ref[0])

    @pl.when(part > 0)
    def other():
        grad = (dk0_ref[0].astype(f32) + dk1_ref[0].astype(f32) + dk2_ref[0].astype(f32)).astype(bf16)
        dkv_ref[0] = grad
        out_ref[0] = dot(normed_ref[...], grad, TN).astype(bf16)
        sums_ref[0] = column_sums(grad.astype(f32))


def weight_grads(normed, dq, parts):
    total, width = normed.shape
    lanes = dq.shape[1]
    before = lambda j: (jnp.maximum(j - 1, 0), 0, 0)
    part = pl.BlockSpec((1, total, lanes), before)
    return pl.pallas_call(
        weight_kernel,
        grid=(3,),
        in_specs=[full((total, width)), full((total, lanes)), part, part, part],
        out_specs=[
            pl.BlockSpec((1, width, lanes), lambda j: (j, 0, 0)),
            part,
            pl.BlockSpec((1, 1, lanes), lambda j: (j, 0, 0)),
        ],
        out_shape=[
            jax.ShapeDtypeStruct((3, width, lanes), bf16),
            jax.ShapeDtypeStruct((2, total, lanes), bf16),
            jax.ShapeDtypeStruct((3, 1, lanes), f32),
        ],
        compiler_params=params(),
        cost_estimate=pl.CostEstimate(
            flops=6 * total * width * lanes, bytes_accessed=8_000_000, transcendentals=0
        ),
        name="weight_grads",
    )(normed, dq, *parts)


def input_kernel(counts, groups, *refs):
    clips, slots, rows = counts
    dqs = refs[:groups]
    dkvs = refs[groups : 2 * groups]
    qkv_ref, tok_ref, gmid_ref, gain_ref, shift_ref, out_ref, small_ref = refs[2 * groups :]
    clip = pl.program_id(0)
    width = tok_ref.shape[-1]
    lanes = width // groups
    grad = None
    for group in range(groups):
        for part in range(3):
            rows_grad = dqs[group][0] if part == 0 else dkvs[group][part - 1]
            at = part * width + group * lanes
            more = dot(rows_grad, qkv_ref[:, at : at + lanes], NT)
            grad = more if grad is None else grad + more
    unit, inverse = center_scale(tok_ref[0].astype(f32))
    result = gmid_ref[0] + norm_back(unit, inverse, gain_ref[...], grad)
    out_ref[0] = result[:slots]

    @pl.when(clip == 0)
    def start():
        small_ref[...] = jnp.zeros_like(small_ref)

    small_ref[0:1] += column_sums(grad * unit)
    small_ref[1:2] += column_sums(grad)


def input_grads(dqs, dkvs, qkv_weight, tokens, gmid, gain, shift, slots):
    clips, rows, width = tokens.shape
    groups = len(dqs)
    lanes = width // groups
    tok = pl.BlockSpec((1, rows, width), lambda c: (c, 0, 0))
    return pl.pallas_call(
        functools.partial(input_kernel, (clips, slots, rows), groups),
        grid=(clips,),
        in_specs=[pl.BlockSpec((1, rows, lanes), lambda c: (c, 0, 0))] * groups
        + [pl.BlockSpec((2, rows, lanes), lambda c: (0, c, 0))] * groups
        + [full(qkv_weight.shape), tok, tok, full((1, width)), full((1, width))],
        out_specs=[pl.BlockSpec((1, slots, width), lambda c: (c, 0, 0)), full((8, width))],
        out_shape=[
            jax.ShapeDtypeStruct((clips, slots, width), f32),
            jax.ShapeDtypeStruct((8, width), f32),
        ],
        compiler_params=params(),
        cost_estimate=pl.CostEstimate(
            flops=6 * clips * rows * width * width, bytes_accessed=16_000_000, transcendentals=0
        ),
        name="input_grads",
    )(*dqs, *dkvs, qkv_weight, tokens, gmid, gain, shift)


def swap_bit(array, axis, size, bit):
    return lax.ppermute(array, axis, [(i, i ^ (1 << bit)) for i in range(size)])


def add_low(left, right):
    return (left.astype(f32) + right.astype(f32)).astype(bf16)


def pick(array, index, dim):
    return lax.dynamic_index_in_dim(array, index, dim, keepdims=False)


def bit_of(axis, bit):
    return (lax.axis_index(axis) >> bit) & 1


def scatter_sum(split, clip_size, order):
    core = bit_of("freq", 0)
    vert = bit_of("freq", 1)
    bits = clip_size.bit_length() - 1
    lanes = split.shape[-1]
    value = add_low(pick(split, core, 0), swap_bit(pick(split, 1 - core, 0), "freq", 4, 0))
    rows = value.shape[0] // (2 * clip_size)
    value = value.reshape((2,) * bits + (2, rows, lanes))
    left = list(range(bits))[::-1]
    for bit in order:
        at = left.index(bit)
        mine = bit_of("clip", bit)
        value = add_low(
            pick(value, mine, at), swap_bit(pick(value, 1 - mine, at), "clip", clip_size, bit)
        )
        left.remove(bit)
    return add_low(pick(value, vert, 0), swap_bit(pick(value, 1 - vert, 0), "freq", 4, 1))


def gather_low(part):
    core = bit_of("freq", 0)
    vert = bit_of("freq", 1)
    other = swap_bit(part, "freq", 4, 1)
    tall = jnp.where(vert == 0, jnp.concatenate([part, other]), jnp.concatenate([other, part]))
    side = swap_bit(tall, "freq", 4, 0)
    return jnp.where(
        core == 0,
        jnp.concatenate([tall, side], axis=1),
        jnp.concatenate([side, tall], axis=1),
    ).astype(f32)


def total_sum(array, clip_size):
    for bit in range(2):
        array = array + swap_bit(array, "freq", 4, bit)
    for bit in range(clip_size.bit_length() - 1):
        array = array + swap_bit(array, "clip", clip_size, bit)
    return array


def on_device(
    clip_size, tokens, kept_counts, attn_gain, attn_shift, qkv_weight, query_bias, value_bias,
    proj_weight, proj_bias, mlp_gain, mlp_shift, fc1_weight, fc1_bias, fc2_weight, fc2_bias, cotangent,
):
    clips, slots, width = tokens.shape
    rows = -(-slots // 16) * 16
    total = clips * rows
    bits = clip_size.bit_length() - 1
    forward_order = list(range(bits))
    second_order = forward_order[1:2] + forward_order[:1] + forward_order[2:]
    pad = ((0, 0), (0, rows - slots), (0, 0))
    vec = lambda v: v.astype(f32)[None, :]
    slot_ids = jnp.arange(rows, dtype=jnp.int32)
    live = (slot_ids[None, :] < kept_counts).astype(f32).reshape(total, 1)
    kept = (kept_counts - slots // 2).astype(bf16)
    tok = jnp.concatenate(
        [tokens, jnp.broadcast_to(kept[:, :, None], (clips, rows - slots, width))], axis=1
    )
    vectors = [vec(v) for v in (query_bias, value_bias, attn_gain, attn_shift, proj_bias, mlp_gain, mlp_shift)]
    q, k, v, normed, mixed, lse, middle, normed2, mask = forward(
        tok, slots, qkv_weight, vectors, proj_weight
    )
    flat = lambda a: a.reshape(total, width)
    cot = jnp.pad(cotangent, pad)
    layer_out, dfc1, dfc2, dproj, db1, small2, gmid, gmixed = mlp(
        flat(normed2), flat(middle), flat(cot), live, flat(mixed), fc1_weight, vec(fc1_bias),
        fc2_weight, vec(fc2_bias), vectors[5], vectors[6], proj_weight, (clips, slots, rows),
    )
    early = total_sum(jnp.concatenate([small2[:4].reshape(-1), db1.reshape(-1)])[None, :], clip_size)[0]
    sum_fc1 = gather_low(scatter_sum(dfc1, clip_size, forward_order))
    sum_fc2 = gather_low(scatter_sum(dfc2, clip_size, second_order))
    sum_proj = gather_low(scatter_sum(dproj, clip_size, forward_order))

    groups = 3
    pairs = HEADS // 2 // groups
    lanes = pairs * 2 * DH
    gmixed = gmixed.reshape(clips, rows, width)
    dqs, dkvs, sums, sharded = [], [], [], []
    for group in range(groups):
        dq, keep, send = attend_back(q, k, v, mask, mixed, lse, gmixed, group * pairs, pairs)
        got = swap_bit(send, "freq", 4, 0)
        across = swap_bit(add_low(keep[:, :, rows:], got[:, :, rows:]), "freq", 4, 1)
        parts = [a.reshape(2, total, lanes) for a in (keep[:, :, :rows], got[:, :, :rows], across)]
        dw, dkv, colsum = weight_grads(flat(normed), dq.reshape(total, lanes), parts)
        half = lanes // 2
        split = jnp.stack(
            [
                jnp.concatenate([dw[i, :, s * half : (s + 1) * half] for i in range(3)], axis=1)
                for s in range(2)
            ]
        )
        order = forward_order if group % 2 == 0 else second_order
        summed = gather_low(scatter_sum(split, clip_size, order))
        sharded.append(summed.reshape(summed.shape[0], 2, 3, half))
        dqs.append(dq)
        dkvs.append(dkv)
        sums.append(colsum)
    grad_tokens, small1 = input_grads(
        dqs, dkvs, qkv_weight, tok, gmid.reshape(clips, rows, width), vectors[2], vectors[3], slots
    )
    qkv = jnp.stack(sharded, axis=1)
    sum_qkv = qkv.transpose(0, 3, 1, 2, 4).reshape(qkv.shape[0], 3 * width)
    bias = jnp.concatenate(sums, axis=2)
    late = total_sum(
        jnp.concatenate([small1[0:1], small1[1:2], bias[0], bias[2]], axis=1), clip_size
    )[0]
    cut = lambda a, i: a[i * width : (i + 1) * width]
    return (
        layer_out, grad_tokens, cut(late, 0), cut(late, 1), sum_qkv, cut(late, 2), cut(late, 3),
        sum_proj, cut(early, 3), cut(early, 0), cut(early, 1), sum_fc1, early[4 * width :],
        sum_fc2, cut(early, 2),
    )


def solution(mesh):
    rows = P("clip", "freq", None)
    shard = P("clip", None)
    return jax.shard_map(
        functools.partial(on_device, mesh.shape["clip"]),
        mesh=mesh,
        in_specs=(rows, P("clip", "freq")) + (P(),) * 13 + (rows,),
        out_specs=(rows, rows, P(), P(), shard, P(), P(), shard, P(), P(), P(), shard, P(), shard, P()),
        check_vma=False,
    )
```

profile of v0, /device:TPU:0, one launch (start us, length us, event | category | flops | bytes accessed | tf_op | source)
XLA Modules:
  0.0 441.7 jit_solution(9128001939178382844)
XLA Ops:
  14.5 2.7 pad_maximum_fusion.tok_ref.refs_7_
  18.4 72.1 %forward.1 = (bf16[3,304,768]{2,1,0:T(8,128)(2,1)}, bf16[3,1216,768]{2,1,0:T(8,128)(2,1)}, bf16[3,1216,768]{2,1,0:T(8,128)(2,1)}, bf16[3,304,768]{2,1,0:T(8,128)...) custom-call(bf16[3,304,768]{2,1,0:T(8,128)(2,1)} %pad_maximum_fusion, ...), custom_call_target="tpu_custom_call" | custom-call | flops 14165213184 | bytes 40000000 | tf_op jit(solution)/shard_map/forward/pallas_call | solution.py:185
  90.4 51.7 %mlp.1 = (bf16[3,298,768]{2,1,0:T(8,128)(2,1)}, bf16[2,768,1536]{2,1,0:T(8,128)(2,1)}, bf16[2,3072,384]{2,1,0:T(8,128)(2,1)}, bf16[2,768,384]{2,1,0:T(8,128)(2,1...) custom-call(bf16[912,768]{1,0:T(8,128)(2,1)} %bitcast.299, ...), custom_call_target="tpu_custom_call" | custom-call | flops 25820135424 | bytes 40000000 | tf_op jit(solution)/shard_map/mlp/pallas_call | solution.py:309
  142.1 3.4 dynamic-slice_bitcast_fusion
  146.1 17.9 %attend_back.3 = (bf16[3,304,256]{2,1,0:T(8,128)(2,1)}, bf16[2,3,608,256]{3,2,1,0:T(8,128)(2,1)}, bf16[2,3,608,256]{3,2,1,0:T(8,128)(2,1)}) custom-call(bf16[3,304,768]{2,1,0:T(8,128)(2,1)} %get-tuple-element.56.q_ref, bf16[3,1216,768]{2,1,0:T(8,128)(2,1)} %get-tuple-element.57.k_ref, bf16[3,1216,768]{2,1,0:T(8,128)(2,1)} %get-tuple-element.58.v_ref, ...), custom_call_target="tpu_custom_call" | custom-call | flops 11356078080 | bytes 12140544 | tf_op jit(solution)/shard_map/attend_back/pallas_call | solution.py:397
  164.1 17.8 %attend_back.4 = (bf16[3,304,256]{2,1,0:T(8,128)(2,1)}, bf16[2,3,608,256]{3,2,1,0:T(8,128)(2,1)}, bf16[2,3,608,256]{3,2,1,0:T(8,128)(2,1)}) custom-call(bf16[3,304,768]{2,1,0:T(8,128)(2,1)} %get-tuple-element.56.q_ref, bf16[3,1216,768]{2,1,0:T(8,128)(2,1)} %get-tuple-element.57.k_ref, bf16[3,1216,768]{2,1,0:T(8,128)(2,1)} %get-tuple-element.58.v_ref, ...), custom_call_target="tpu_custom_call" | custom-call | flops 11356078080 | bytes 12140544 | tf_op jit(solution)/shard_map/attend_back/pallas_call | solution.py:397
  182.4 2.1 collective-permute-start.40
  184.6 18.0 %attend_back.5 = (bf16[3,304,256]{2,1,0:T(8,128)(2,1)}, bf16[2,3,608,256]{3,2,1,0:T(8,128)(2,1)}, bf16[2,3,608,256]{3,2,1,0:T(8,128)(2,1)}) custom-call(bf16[3,304,768]{2,1,0:T(8,128)(2,1)} %get-tuple-element.56.q_ref, bf16[3,1216,768]{2,1,0:T(8,128)(2,1)} %get-tuple-element.57.k_ref, bf16[3,1216,768]{2,1,0:T(8,128)(2,1)} %get-tuple-element.58.v_ref, ...), custom_call_target="tpu_custom_call" | custom-call | flops 11356078080 | bytes 12140544 | tf_op jit(solution)/shard_map/attend_back/pallas_call | solution.py:397
  203.9 2.7 collective-permute-done.41
  207.9 2.7 collective-permute-done.42
  210.6 2.2 collective-permute-start.43
  212.9 2.5 collective-permute-done.43
  216.0 3.2 dynamic-slice_bitcast_fusion.1
  219.2 2.4 slice.159
  228.8 2.5 add_convert_fusion.1
  231.3 1.9 collective-permute-start.3
  233.2 2.4 add_convert_fusion
  235.8 2.2 slice.212
  237.9 2.2 slice.214
  240.1 2.3 slice.216
  245.9 2.3 fusion.1
  252.2 5.6 %weight_grads.3 = (bf16[3,768,256]{2,1,0:T(8,128)(2,1)}, bf16[2,912,256]{2,1,0:T(8,128)(2,1)}, f32[3,1,256]{2,1,0:T(1,128)}) custom-call(bf16[912,768]{1,0:T(8,128)(2,1)} %bitcast.260, bf16[912,256]{1,0:T(8,128)(2,1)} %bitcast.280, bf16[2,912,256]{2,1,0:T(8,128)(2,1)} %bitcast.271, bf16[2,912,256]{2,1,0:T(8,128)(2,1)} %bitcast.274, ...), custom_call_target="tpu_custom_call" | custom-call | flops 1075838976 | bytes 8000000 | tf_op jit(solution)/shard_map/weight_grads/pallas_call | solution.py:439
  260.5 11.8 %collective-permute-done.3 = bf16[2,3,304,256]{3,2,1,0:T(8,128)(2,1)} collective-permute-done((bf16[2,3,304,256]{3,2,1,0:T(8,128)(2,1)}, bf16[2,3,304,256]{3,2,1,0:T(8,128)(2,1)}, u32[]{:S(2)}, u32[]{:S(2)}) %collective-permute-start.3) | collective-permute-done | bytes 933920 | tf_op jit(solution)/shard_map/ppermute | solution.py:513
  272.2 5.6 %weight_grads.4 = (bf16[3,768,256]{2,1,0:T(8,128)(2,1)}, bf16[2,912,256]{2,1,0:T(8,128)(2,1)}, f32[3,1,256]{2,1,0:T(1,128)}) custom-call(bf16[912,768]{1,0:T(8,128)(2,1)} %bitcast.261, bf16[912,256]{1,0:T(8,128)(2,1)} %bitcast.281, bf16[2,912,256]{2,1,0:T(8,128)(2,1)} %bitcast.270, bf16[2,912,256]{2,1,0:T(8,128)(2,1)} %bitcast.273, ...), custom_call_target="tpu_custom_call" | custom-call | flops 1075838976 | bytes 8000000 | tf_op jit(solution)/shard_map/weight_grads/pallas_call | solution.py:439
  280.4 2.4 slice_bitcast_fusion.8
  282.7 9.1 %collective-permute-done.5 = bf16[2,3,304,256]{3,2,1,0:T(8,128)(2,1)} collective-permute-done((bf16[2,3,304,256]{3,2,1,0:T(8,128)(2,1)}, bf16[2,3,304,256]{3,2,1,0:T(8,128)(2,1)}, u32[]{:S(2)}, u32[]{:S(2)}) %collective-permute-start.5) | collective-permute-done | bytes 933920 | tf_op jit(solution)/shard_map/ppermute | solution.py:513
  291.9 5.6 %weight_grads.5 = (bf16[3,768,256]{2,1,0:T(8,128)(2,1)}, bf16[2,912,256]{2,1,0:T(8,128)(2,1)}, f32[3,1,256]{2,1,0:T(1,128)}) custom-call(bf16[912,768]{1,0:T(8,128)(2,1)} %bitcast.262, bf16[912,256]{1,0:T(8,128)(2,1)} %bitcast.282, bf16[2,912,256]{2,1,0:T(8,128)(2,1)} %bitcast.269, bf16[2,912,256]{2,1,0:T(8,128)(2,1)} %bitcast.272, ...), custom_call_target="tpu_custom_call" | custom-call | flops 1075838976 | bytes 8000000 | tf_op jit(solution)/shard_map/weight_grads/pallas_call | solution.py:439
  300.0 9.5 %input_grads.1 = (f32[3,298,768]{2,1,0:T(8,128)}, f32[8,768]{1,0:T(8,128)}) custom-call(bf16[3,304,256]{2,1,0:T(8,128)(2,1)} %get-tuple-element.62.refs_0_, bf16[3,304,256]{2,1,0:T(8,128)(2,1)} %get-tuple-element.63.refs_1_, bf16[3,304,256]{2,1,0:T(8,128)(2,1)} %get-tuple-element.64.refs_2_, bf16[2,912,256]{2,1,0:T(8,128)(2,1)} %get-tuple-element.68.refs_3_, ...), custom_call_target="tpu_custom_call" | custom-call | flops 3227516928 | bytes 16000000 | tf_op jit(solution)/shard_map/input_grads/pallas_call | solution.py:493
  313.6 2.9 collective-permute-done.7
  317.9 2.4 collective-permute-done.8
  321.7 2.4 collective-permute-done.9
  324.1 2.3 collective-permute-start.10
  326.6 2.2 collective-permute-done.10
  342.1 5.0 %collective-permute-done.12 = bf16[2,2,2,48,384]{4,3,2,0,1:T(8,128)(2,1)S(1)} collective-permute-done((bf16[2,2,2,48,384]{4,3,2,0,1:T(8,128)(2,1)S(1)}, bf16[2,2,2,48,384]{4,3,2,0,1:T(8,128)(2,1)S(1)}, u32[]{:S(2)}, u32[]{:S(2)}) %collective-permute-start.12) | collective-permute-done | bytes 294944 | tf_op jit(solution)/shard_map/ppermute | solution.py:513
  349.4 4.0 collective-permute-done.26
  354.6 5.6 %collective-permute-done.34 = bf16[2,2,48,384]{3,2,1,0:T(8,128)(2,1)S(1)} collective-permute-done((bf16[2,2,48,384]{3,2,1,0:T(8,128)(2,1)S(1)}, bf16[2,2,48,384]{3,2,1,0:T(8,128)(2,1)S(1)}, u32[]{:S(2)}, u32[]{:S(2)}) %collective-permute-start.34) | collective-permute-done | bytes 147488 | tf_op jit(solution)/shard_map/ppermute | solution.py:513
  363.3 2.8 collective-permute-start.35
  366.1 2.7 collective-permute-done.20
  368.8 2.2 collective-permute-start.14
  372.0 2.3 collective-permute-start.28
  374.3 4.6 %collective-permute-done.14 = bf16[2,48,384]{2,1,0:T(8,128)(2,1)S(1)} collective-permute-done((bf16[2,48,384]{2,1,0:T(8,128)(2,1)S(1)}, bf16[2,48,384]{2,1,0:T(8,128)(2,1)S(1)}, u32[]{:S(2)}, u32[]{:S(2)}) %collective-permute-start.14) | collective-permute-done | bytes 73760 | tf_op jit(solution)/shard_map/ppermute | solution.py:513
  391.0 2.0 collective-permute-done.30
  394.8 3.0 collective-permute-start.47
  397.8 19.2 %collective-permute-done.54 = bf16[2,192,384]{2,1,0:T(8,128)(2,1)S(1)} collective-permute-done((bf16[2,192,384]{2,1,0:T(8,128)(2,1)S(1)}, bf16[2,192,384]{2,1,0:T(8,128)(2,1)S(1)}, u32[]{:S(2)}, u32[]{:S(2)}) %collective-permute-start.54) | collective-permute-done | bytes 294944 | tf_op jit(solution)/shard_map/ppermute | solution.py:513
  417.6 5.6 %collective-permute-done.47 = bf16[2,48,1536]{2,1,0:T(8,128)(2,1)S(1)} collective-permute-done((bf16[2,48,1536]{2,1,0:T(8,128)(2,1)S(1)}, bf16[2,48,1536]{2,1,0:T(8,128)(2,1)S(1)}, u32[]{:S(2)}, u32[]{:S(2)}) %collective-permute-start.47) | collective-permute-done | bytes 294944 | tf_op jit(solution)/shard_map/ppermute | solution.py:513
  425.5 4.6 %collective-permute-done.48 = bf16[48,1536]{1,0:T(8,128)(2,1)S(1)} collective-permute-done((bf16[48,1536]{1,0:T(8,128)(2,1)S(1)}, bf16[48,1536]{1,0:T(8,128)(2,1)S(1)}, u32[]{:S(2)}, u32[]{:S(2)}) %collective-permute-start.48) | collective-permute-done | bytes 147488 | tf_op jit(solution)/shard_map/ppermute | solution.py:513
  430.9 2.3 collective-permute-done.56
  433.4 2.1 collective-permute-done.49
  (255 shorter events, 93.1 us)
Async XLA Ops:
  145.5 97.0 %collective-permute-start.51 = (bf16[3072,384]{1,0:T(8,128)(2,1)}, bf16[3072,384]{1,0:T(8,128)(2,1)S(1)}, u32[]{:S(2)}, u32[]{:S(2)}) collective-permute-start(bf16[3072,384]{1,0:T(8,128)(2,1)} %dynamic-slice_bitcast_fusion), channel_id=1, source_target_pairs={{0,1},{1,0},{2,3},{3,2},{4,5},{5,4},{6,7},{7,6},{8,9},{9,8},{10,11... | collective-permute-start | bytes 7077896 | tf_op jit(solution)/shard_map/ppermute | solution.py:513
  145.6 36.8 %collective-permute-start.39 = (f32[1,6144]{1,0:T(1,128)S(1)}, f32[1,6144]{1,0:T(1,128)S(1)}, u32[]{:S(2)}, u32[]{:S(2)}) collective-permute-start(f32[1,6144]{1,0:T(1,128)S(1)} %bitcast.288), channel_id=1, source_target_pairs={{0,1},{1,0},{2,3},{3,2},{4,5},{5,4},{6,7},{7,6},{8,9},{9,8},{10,11... | collective-permute-start | bytes 73736 | tf_op jit(solution)/shard_map/ppermute | solution.py:513
  164.1 62.9 %collective-permute-start = (bf16[2,3,608,256]{3,2,1,0:T(8,128)(2,1)}, bf16[2,3,608,256]{3,2,1,0:T(8,128)(2,1)}, u32[]{:S(2)}, u32[]{:S(2)}) collective-permute-start(bf16[2,3,608,256]{3,2,1,0:T(8,128)(2,1)} %get-tuple-element.67), channel_id=1, source_target_pairs={{0,1},{1,0},{2,3},{3,2},{4,5},{5,4},{6,7},{7,6},{8,9},{9,8},{10,11... | collective-permute-start | bytes 5603336 | tf_op jit(solution)/shard_map/ppermute | solution.py:513
  181.9 46.8 %collective-permute-start.2 = (bf16[2,3,608,256]{3,2,1,0:T(8,128)(2,1)}, bf16[2,3,608,256]{3,2,1,0:T(8,128)(2,1)}, u32[]{:S(2)}, u32[]{:S(2)}) collective-permute-start(bf16[2,3,608,256]{3,2,1,0:T(8,128)(2,1)} %get-tuple-element.70), channel_id=1, source_target_pairs={{0,1},{1,0},{2,3},{3,2},{4,5},{5,4},{6,7},{7,6},{8,9},{9,8},{10,11... | collective-permute-start | bytes 5603336 | tf_op jit(solution)/shard_map/ppermute | solution.py:513
  182.4 20.2 %collective-permute-start.40 = (f32[1,6144]{1,0:T(1,128)S(1)}, f32[1,6144]{1,0:T(1,128)S(1)}, u32[]{:S(2)}, u32[]{:S(2)}) collective-permute-start(f32[1,6144]{1,0:T(1,128)S(1)} %add.271), channel_id=1, source_target_pairs={{0,2},{1,3},{2,0},{3,1},{4,6},{5,7},{6,4},{7,5},{8,10},{9,11},{10,... | collective-permute-start | bytes 73736 | tf_op jit(solution)/shard_map/ppermute | solution.py:513
  202.6 30.6 %collective-permute-start.4 = (bf16[2,3,608,256]{3,2,1,0:T(8,128)(2,1)}, bf16[2,3,608,256]{3,2,1,0:T(8,128)(2,1)}, u32[]{:S(2)}, u32[]{:S(2)}) collective-permute-start(bf16[2,3,608,256]{3,2,1,0:T(8,128)(2,1)} %get-tuple-element.73), channel_id=1, source_target_pairs={{0,1},{1,0},{2,3},{3,2},{4,5},{5,4},{6,7},{7,6},{8,9},{9,8},{10,11... | collective-permute-start | bytes 5603336 | tf_op jit(solution)/shard_map/ppermute | solution.py:513
  210.6 4.8 %collective-permute-start.43 = (f32[1,6144]{1,0:T(1,128)S(1)}, f32[1,6144]{1,0:T(1,128)S(1)}, u32[]{:S(2)}, u32[]{:S(2)}) collective-permute-start(f32[1,6144]{1,0:T(1,128)S(1)} %add.274), channel_id=1, source_target_pairs={{0,16},{4,20},{8,24},{12,28},{16,0},{20,4},{24,8},{28,12},{1,17},{... | collective-permute-start | bytes 73736 | tf_op jit(solution)/shard_map/ppermute | solution.py:513
  219.2 26.7 %collective-permute-start.44 = (bf16[768,1536]{1,0:T(8,128)(2,1)}, bf16[768,1536]{1,0:T(8,128)(2,1)}, u32[]{:S(2)}, u32[]{:S(2)}) collective-permute-start(bf16[768,1536]{1,0:T(8,128)(2,1)} %dynamic-slice_bitcast_fusion.1), channel_id=1, source_target_pairs={{0,1},{1,0},{2,3},{3,2},{4,5},{5,4},{6,7},{7,6},{8,9},{9,8},{10,11... | collective-permute-start | bytes 7077896 | tf_op jit(solution)/shard_map/ppermute | solution.py:513
  228.6 23.7 %collective-permute-start.1 = (bf16[2,3,304,256]{3,2,1,0:T(8,128)(2,1)S(1)}, bf16[2,3,304,256]{3,2,1,0:T(8,128)(2,1)}, u32[]{:S(2)}, u32[]{:S(2)}) collective-permute-start(bf16[2,3,304,256]{3,2,1,0:T(8,128)(2,1)S(1)} %add_convert_fusion.2), channel_id=1, source_target_pairs={{0,2},{1,3},{2,0},{3,1},{4,6},{5,7},{6,4},{7,5},{8,10},{9,11},{10,... | collective-permute-start | bytes 2801672 | tf_op jit(solution)/shard_map/ppermute | solution.py:513
  231.3 40.9 %collective-permute-start.3 = (bf16[2,3,304,256]{3,2,1,0:T(8,128)(2,1)}, bf16[2,3,304,256]{3,2,1,0:T(8,128)(2,1)}, u32[]{:S(2)}, u32[]{:S(2)}) collective-permute-start(bf16[2,3,304,256]{3,2,1,0:T(8,128)(2,1)} %add_convert_fusion.1), channel_id=1, source_target_pairs={{0,2},{1,3},{2,0},{3,1},{4,6},{5,7},{6,4},{7,5},{8,10},{9,11},{10,... | collective-permute-start | bytes 2801672 | tf_op jit(solution)/shard_map/ppermute | solution.py:513
  235.6 56.3 %collective-permute-start.5 = (bf16[2,3,304,256]{3,2,1,0:T(8,128)(2,1)}, bf16[2,3,304,256]{3,2,1,0:T(8,128)(2,1)}, u32[]{:S(2)}, u32[]{:S(2)}) collective-permute-start(bf16[2,3,304,256]{3,2,1,0:T(8,128)(2,1)} %add_convert_fusion), channel_id=1, source_target_pairs={{0,2},{1,3},{2,0},{3,1},{4,6},{5,7},{6,4},{7,5},{8,10},{9,11},{10,... | collective-permute-start | bytes 2801672 | tf_op jit(solution)/shard_map/ppermute | solution.py:513
  244.5 90.7 %collective-permute-start.52 = (bf16[2,2,2,192,384]{4,3,2,0,1:T(8,128)(2,1)}, bf16[2,2,2,192,384]{4,3,2,0,1:T(8,128)(2,1)}, u32[]{:S(2)}, u32[]{:S(2)}) collective-permute-start(bf16[2,2,2,192,384]{4,3,2,0,1:T(8,128)(2,1)} %bitcast.254), channel_id=1, source_target_pairs={{0,8},{4,12},{8,0},{12,4},{16,24},{20,28},{24,16},{28,20},{1,9},{5... | collective-permute-start | bytes 3538952 | tf_op jit(solution)/shard_map/ppermute | solution.py:513
  249.5 88.9 %collective-permute-start.45 = (bf16[2,2,2,48,1536]{4,3,2,0,1:T(8,128)(2,1)}, bf16[2,2,2,48,1536]{4,3,2,0,1:T(8,128)(2,1)}, u32[]{:S(2)}, u32[]{:S(2)}) collective-permute-start(bf16[2,2,2,48,1536]{4,3,2,0,1:T(8,128)(2,1)} %bitcast.255), channel_id=1, source_target_pairs={{0,4},{4,0},{8,12},{12,8},{16,20},{20,16},{24,28},{28,24},{1,5},{5... | collective-permute-start | bytes 3538952 | tf_op jit(solution)/shard_map/ppermute | solution.py:513
  260.5 68.9 %collective-permute-start.11 = (bf16[768,384]{1,0:T(8,128)(2,1)}, bf16[768,384]{1,0:T(8,128)(2,1)}, u32[]{:S(2)}, u32[]{:S(2)}) collective-permute-start(bf16[768,384]{1,0:T(8,128)(2,1)} %fusion.19), channel_id=1, source_target_pairs={{0,1},{1,0},{2,3},{3,2},{4,5},{5,4},{6,7},{7,6},{8,9},{9,8},{10,11... | collective-permute-start | bytes 1769480 | tf_op jit(solution)/shard_map/ppermute | solution.py:513
  313.3 18.8 %collective-permute-start.18 = (bf16[768,384]{1,0:T(8,128)(2,1)S(1)}, bf16[768,384]{1,0:T(8,128)(2,1)S(1)}, u32[]{:S(2)}, u32[]{:S(2)}) collective-permute-start(bf16[768,384]{1,0:T(8,128)(2,1)S(1)} %fusion.15), channel_id=1, source_target_pairs={{0,1},{1,0},{2,3},{3,2},{4,5},{5,4},{6,7},{7,6},{8,9},{9,8},{10,11... | collective-permute-start | bytes 1769480 | tf_op jit(solution)/shard_map/ppermute | solution.py:513
  324.1 4.7 %collective-permute-start.10 = (f32[1,3072]{1,0:T(1,128)S(1)}, f32[1,3072]{1,0:T(1,128)S(1)}, u32[]{:S(2)}, u32[]{:S(2)}) collective-permute-start(f32[1,3072]{1,0:T(1,128)S(1)} %add.239), channel_id=1, source_target_pairs={{0,16},{4,20},{8,24},{12,28},{16,0},{20,4},{24,8},{28,12},{1,17},{... | collective-permute-start | bytes 36872 | tf_op jit(solution)/shard_map/ppermute | solution.py:513
  328.7 4.8 %collective-permute-start.25 = (bf16[768,384]{1,0:T(8,128)(2,1)S(1)}, bf16[768,384]{1,0:T(8,128)(2,1)S(1)}, u32[]{:S(2)}, u32[]{:S(2)}) collective-permute-start(bf16[768,384]{1,0:T(8,128)(2,1)S(1)} %fusion.11), channel_id=1, source_target_pairs={{0,1},{1,0},{2,3},{3,2},{4,5},{5,4},{6,7},{7,6},{8,9},{9,8},{10,11... | collective-permute-start | bytes 1769480 | tf_op jit(solution)/shard_map/ppermute | solution.py:513
  330.9 9.9 %collective-permute-start.33 = (bf16[2,2,2,48,384]{4,3,2,0,1:T(8,128)(2,1)S(1)}, bf16[2,2,2,48,384]{4,3,2,0,1:T(8,128)(2,1)S(1)}, u32[]{:S(2)}, u32[]{:S(2)}) collective-permute-start(bf16[2,2,2,48,384]{4,3,2,0,1:T(8,128)(2,1)S(1)} %bitcast.286), channel_id=1, source_target_pairs={{0,4},{4,0},{8,12},{12,8},{16,20},{20,16},{24,28},{28,24},{1,5},{5... | collective-permute-start | bytes 884744 | tf_op jit(solution)/shard_map/ppermute | solution.py:513
  332.1 15.0 %collective-permute-start.12 = (bf16[2,2,2,48,384]{4,3,2,0,1:T(8,128)(2,1)S(1)}, bf16[2,2,2,48,384]{4,3,2,0,1:T(8,128)(2,1)S(1)}, u32[]{:S(2)}, u32[]{:S(2)}) collective-permute-start(bf16[2,2,2,48,384]{4,3,2,0,1:T(8,128)(2,1)S(1)} %bitcast.284), channel_id=1, source_target_pairs={{0,4},{4,0},{8,12},{12,8},{16,20},{20,16},{24,28},{28,24},{1,5},{5... | collective-permute-start | bytes 884744 | tf_op jit(solution)/shard_map/ppermute | solution.py:513
  333.6 14.8 %collective-permute-start.19 = (bf16[2,2,2,48,384]{4,3,2,0,1:T(8,128)(2,1)S(1)}, bf16[2,2,2,48,384]{4,3,2,0,1:T(8,128)(2,1)S(1)}, u32[]{:S(2)}, u32[]{:S(2)}) collective-permute-start(bf16[2,2,2,48,384]{4,3,2,0,1:T(8,128)(2,1)S(1)} %bitcast.285), channel_id=1, source_target_pairs={{0,8},{4,12},{8,0},{12,4},{16,24},{20,28},{24,16},{28,20},{1,9},{5... | collective-permute-start | bytes 884744 | tf_op jit(solution)/shard_map/ppermute | solution.py:513
  335.2 18.2 %collective-permute-start.26 = (bf16[2,2,2,48,384]{4,3,2,0,1:T(8,128)(2,1)S(1)}, bf16[2,2,2,48,384]{4,3,2,0,1:T(8,128)(2,1)S(1)}, u32[]{:S(2)}, u32[]{:S(2)}) collective-permute-start(bf16[2,2,2,48,384]{4,3,2,0,1:T(8,128)(2,1)S(1)} %bitcast.287), channel_id=1, source_target_pairs={{0,4},{4,0},{8,12},{12,8},{16,20},{20,16},{24,28},{28,24},{1,5},{5... | collective-permute-start | bytes 884744 | tf_op jit(solution)/shard_map/ppermute | solution.py:513
  338.4 55.8 %collective-permute-start.53 = (bf16[2,2,192,384]{3,2,1,0:T(8,128)(2,1)S(1)}, bf16[2,2,192,384]{3,2,1,0:T(8,128)(2,1)S(1)}, u32[]{:S(2)}, u32[]{:S(2)}) collective-permute-start(bf16[2,2,192,384]{3,2,1,0:T(8,128)(2,1)S(1)} %dynamic-slice_bitcast_fusion.2), channel_id=1, source_target_pairs={{0,4},{4,0},{8,12},{12,8},{16,20},{20,16},{24,28},{28,24},{1,5},{5... | collective-permute-start | bytes 1769480 | tf_op jit(solution)/shard_map/ppermute | solution.py:513
  340.8 53.8 %collective-permute-start.46 = (bf16[2,2,48,1536]{3,2,1,0:T(8,128)(2,1)S(1)}, bf16[2,2,48,1536]{3,2,1,0:T(8,128)(2,1)S(1)}, u32[]{:S(2)}, u32[]{:S(2)}) collective-permute-start(bf16[2,2,48,1536]{3,2,1,0:T(8,128)(2,1)S(1)} %dynamic-slice_bitcast_fusion.3), channel_id=1, source_target_pairs={{0,8},{4,12},{8,0},{12,4},{16,24},{20,28},{24,16},{28,20},{1,9},{5... | collective-permute-start | bytes 1769480 | tf_op jit(solution)/shard_map/ppermute | solution.py:513
  347.1 13.1 %collective-permute-start.34 = (bf16[2,2,48,384]{3,2,1,0:T(8,128)(2,1)S(1)}, bf16[2,2,48,384]{3,2,1,0:T(8,128)(2,1)S(1)}, u32[]{:S(2)}, u32[]{:S(2)}) collective-permute-start(bf16[2,2,48,384]{3,2,1,0:T(8,128)(2,1)S(1)} %dynamic-slice_bitcast_fusion.9), channel_id=1, source_target_pairs={{0,8},{4,12},{8,0},{12,4},{16,24},{20,28},{24,16},{28,20},{1,9},{5... | collective-permute-start | bytes 442376 | tf_op jit(solution)/shard_map/ppermute | solution.py:513
  348.4 14.9 %collective-permute-start.13 = (bf16[2,2,48,384]{3,2,1,0:T(8,128)(2,1)S(1)}, bf16[2,2,48,384]{3,2,1,0:T(8,128)(2,1)S(1)}, u32[]{:S(2)}, u32[]{:S(2)}) collective-permute-start(bf16[2,2,48,384]{3,2,1,0:T(8,128)(2,1)S(1)} %dynamic-slice_bitcast_fusion.12), channel_id=1, source_target_pairs={{0,8},{4,12},{8,0},{12,4},{16,24},{20,28},{24,16},{28,20},{1,9},{5... | collective-permute-start | bytes 442376 | tf_op jit(solution)/shard_map/ppermute | solution.py:513
  353.4 15.4 %collective-permute-start.20 = (bf16[2,2,48,384]{3,2,1,0:T(8,128)(2,1)S(1)}, bf16[2,2,48,384]{3,2,1,0:T(8,128)(2,1)S(1)}, u32[]{:S(2)}, u32[]{:S(2)}) collective-permute-start(bf16[2,2,48,384]{3,2,1,0:T(8,128)(2,1)S(1)} %dynamic-slice_bitcast_fusion.11), channel_id=1, source_target_pairs={{0,4},{4,0},{8,12},{12,8},{16,20},{20,16},{24,28},{28,24},{1,5},{5... | collective-permute-start | bytes 442376 | tf_op jit(solution)/shard_map/ppermute | solution.py:513
  360.2 10.9 %collective-permute-start.27 = (bf16[2,2,48,384]{3,2,1,0:T(8,128)(2,1)S(1)}, bf16[2,2,48,384]{3,2,1,0:T(8,128)(2,1)S(1)}, u32[]{:S(2)}, u32[]{:S(2)}) collective-permute-start(bf16[2,2,48,384]{3,2,1,0:T(8,128)(2,1)S(1)} %dynamic-slice_bitcast_fusion.10), channel_id=1, source_target_pairs={{0,8},{4,12},{8,0},{12,4},{16,24},{20,28},{24,16},{28,20},{1,9},{5... | collective-permute-start | bytes 442376 | tf_op jit(solution)/shard_map/ppermute | solution.py:513
  363.3 8.7 %collective-permute-start.35 = (bf16[2,48,384]{2,1,0:T(8,128)(2,1)S(1)}, bf16[2,48,384]{2,1,0:T(8,128)(2,1)S(1)}, u32[]{:S(2)}, u32[]{:S(2)}) collective-permute-start(bf16[2,48,384]{2,1,0:T(8,128)(2,1)S(1)} %dynamic-slice_bitcast_fusion.13), channel_id=1, source_target_pairs={{0,16},{4,20},{8,24},{12,28},{16,0},{20,4},{24,8},{28,12},{1,17},{... | collective-permute-start | bytes 221192 | tf_op jit(solution)/shard_map/ppermute | solution.py:513
  368.8 10.1 %collective-permute-start.14 = (bf16[2,48,384]{2,1,0:T(8,128)(2,1)S(1)}, bf16[2,48,384]{2,1,0:T(8,128)(2,1)S(1)}, u32[]{:S(2)}, u32[]{:S(2)}) collective-permute-start(bf16[2,48,384]{2,1,0:T(8,128)(2,1)S(1)} %dynamic-slice_bitcast_fusion.16), channel_id=1, source_target_pairs={{0,16},{4,20},{8,24},{12,28},{16,0},{20,4},{24,8},{28,12},{1,17},{... | collective-permute-start | bytes 221192 | tf_op jit(solution)/shard_map/ppermute | solution.py:513
  371.1 9.4 %collective-permute-start.21 = (bf16[2,48,384]{2,1,0:T(8,128)(2,1)S(1)}, bf16[2,48,384]{2,1,0:T(8,128)(2,1)S(1)}, u32[]{:S(2)}, u32[]{:S(2)}) collective-permute-start(bf16[2,48,384]{2,1,0:T(8,128)(2,1)S(1)} %dynamic-slice_bitcast_fusion.15), channel_id=1, source_target_pairs={{0,16},{4,20},{8,24},{12,28},{16,0},{20,4},{24,8},{28,12},{1,17},{... | collective-permute-start | bytes 221192 | tf_op jit(solution)/shard_map/ppermute | solution.py:513
  372.0 9.5 %collective-permute-start.28 = (bf16[2,48,384]{2,1,0:T(8,128)(2,1)S(1)}, bf16[2,48,384]{2,1,0:T(8,128)(2,1)S(1)}, u32[]{:S(2)}, u32[]{:S(2)}) collective-permute-start(bf16[2,48,384]{2,1,0:T(8,128)(2,1)S(1)} %dynamic-slice_bitcast_fusion.14), channel_id=1, source_target_pairs={{0,16},{4,20},{8,24},{12,28},{16,0},{20,4},{24,8},{28,12},{1,17},{... | collective-permute-start | bytes 221192 | tf_op jit(solution)/shard_map/ppermute | solution.py:513
  378.9 4.0 collective-permute-start.36
  380.5 4.3 collective-permute-start.15
  381.5 4.1 collective-permute-start.22
  382.9 4.0 collective-permute-start.29
  384.8 4.2 collective-permute-start.37
  385.6 4.0 collective-permute-start.16
  387.0 4.0 collective-permute-start.23
  389.6 48.6 %collective-permute-start.38 = (bf16[96,384]{1,0:T(8,128)(2,1)S(1)}, bf16[96,384]{1,0:T(8,128)(2,1)S(1)}, u32[]{:S(2)}, u32[]{:S(2)}) collective-permute-start(bf16[96,384]{1,0:T(8,128)(2,1)S(1)} %maximum_select_fusion.11), channel_id=1, source_target_pairs={{0,1},{1,0},{2,3},{3,2},{4,5},{5,4},{6,7},{7,6},{8,9},{9,8},{10,11... | collective-permute-start | bytes 221192 | tf_op jit(solution)/shard_map/ppermute | solution.py:513
  393.0 37.6 %collective-permute-start.31 = (bf16[96,384]{1,0:T(8,128)(2,1)S(1)}, bf16[96,384]{1,0:T(8,128)(2,1)S(1)}, u32[]{:S(2)}, u32[]{:S(2)}) collective-permute-start(bf16[96,384]{1,0:T(8,128)(2,1)S(1)} %maximum_select_fusion.10), channel_id=1, source_target_pairs={{0,1},{1,0},{2,3},{3,2},{4,5},{5,4},{6,7},{7,6},{8,9},{9,8},{10,11... | collective-permute-start | bytes 221192 | tf_op jit(solution)/shard_map/ppermute | solution.py:513
  394.5 22.4 %collective-permute-start.54 = (bf16[2,192,384]{2,1,0:T(8,128)(2,1)S(1)}, bf16[2,192,384]{2,1,0:T(8,128)(2,1)S(1)}, u32[]{:S(2)}, u32[]{:S(2)}) collective-permute-start(bf16[2,192,384]{2,1,0:T(8,128)(2,1)S(1)} %dynamic-slice_bitcast_fusion.5), channel_id=1, source_target_pairs={{0,16},{4,20},{8,24},{12,28},{16,0},{20,4},{24,8},{28,12},{1,17},{... | collective-permute-start | bytes 884744 | tf_op jit(solution)/shard_map/ppermute | solution.py:513
  394.8 28.4 %collective-permute-start.47 = (bf16[2,48,1536]{2,1,0:T(8,128)(2,1)S(1)}, bf16[2,48,1536]{2,1,0:T(8,128)(2,1)S(1)}, u32[]{:S(2)}, u32[]{:S(2)}) collective-permute-start(bf16[2,48,1536]{2,1,0:T(8,128)(2,1)S(1)} %dynamic-slice_bitcast_fusion.6), channel_id=1, source_target_pairs={{0,16},{4,20},{8,24},{12,28},{16,0},{20,4},{24,8},{28,12},{1,17},{... | collective-permute-start | bytes 884744 | tf_op jit(solution)/shard_map/ppermute | solution.py:513
  417.1 6.8 %collective-permute-start.55 = (bf16[192,384]{1,0:T(8,128)(2,1)S(1)}, bf16[192,384]{1,0:T(8,128)(2,1)S(1)}, u32[]{:S(2)}, u32[]{:S(2)}) collective-permute-start(bf16[192,384]{1,0:T(8,128)(2,1)S(1)} %dynamic-slice_bitcast_fusion.7), channel_id=1, source_target_pairs={{0,2},{1,3},{2,0},{3,1},{4,6},{5,7},{6,4},{7,5},{8,10},{9,11},{10,... | collective-permute-start | bytes 442376 | tf_op jit(solution)/shard_map/ppermute | solution.py:513
  423.3 6.8 %collective-permute-start.48 = (bf16[48,1536]{1,0:T(8,128)(2,1)S(1)}, bf16[48,1536]{1,0:T(8,128)(2,1)S(1)}, u32[]{:S(2)}, u32[]{:S(2)}) collective-permute-start(bf16[48,1536]{1,0:T(8,128)(2,1)S(1)} %dynamic-slice_bitcast_fusion.8), channel_id=1, source_target_pairs={{0,2},{1,3},{2,0},{3,1},{4,6},{5,7},{6,4},{7,5},{8,10},{9,11},{10,... | collective-permute-start | bytes 442376 | tf_op jit(solution)/shard_map/ppermute | solution.py:513
  423.9 9.3 %collective-permute-start.56 = (bf16[192,384]{1,0:T(8,128)(2,1)S(1)}, bf16[192,384]{1,0:T(8,128)(2,1)S(1)}, u32[]{:S(2)}, u32[]{:S(2)}) collective-permute-start(bf16[192,384]{1,0:T(8,128)(2,1)S(1)} %fusion.30), channel_id=1, source_target_pairs={{0,2},{1,3},{2,0},{3,1},{4,6},{5,7},{6,4},{7,5},{8,10},{9,11},{10,... | collective-permute-start | bytes 442376 | tf_op jit(solution)/shard_map/ppermute | solution.py:513
  430.1 5.4 %collective-permute-start.49 = (bf16[48,1536]{1,0:T(8,128)(2,1)S(1)}, bf16[48,1536]{1,0:T(8,128)(2,1)S(1)}, u32[]{:S(2)}, u32[]{:S(2)}) collective-permute-start(bf16[48,1536]{1,0:T(8,128)(2,1)S(1)} %fusion.31), channel_id=1, source_target_pairs={{0,2},{1,3},{2,0},{3,1},{4,6},{5,7},{6,4},{7,5},{8,10},{9,11},{10,... | collective-permute-start | bytes 442376 | tf_op jit(solution)/shard_map/ppermute | solution.py:513
  433.3 5.6 %collective-permute-start.57 = (bf16[384,384]{1,0:T(8,128)(2,1)S(1)}, bf16[384,384]{1,0:T(8,128)(2,1)S(1)}, u32[]{:S(2)}, u32[]{:S(2)}) collective-permute-start(bf16[384,384]{1,0:T(8,128)(2,1)S(1)} %maximum_select_fusion.3), channel_id=1, source_target_pairs={{0,1},{1,0},{2,3},{3,2},{4,5},{5,4},{6,7},{7,6},{8,9},{9,8},{10,11... | collective-permute-start | bytes 884744 | tf_op jit(solution)/shard_map/ppermute | solution.py:513
  435.5 4.5 %collective-permute-start.50 = (bf16[96,1536]{1,0:T(8,128)(2,1)S(1)}, bf16[96,1536]{1,0:T(8,128)(2,1)S(1)}, u32[]{:S(2)}, u32[]{:S(2)}) collective-permute-start(bf16[96,1536]{1,0:T(8,128)(2,1)S(1)} %maximum_select_fusion.2), channel_id=1, source_target_pairs={{0,1},{1,0},{2,3},{3,2},{4,5},{5,4},{6,7},{7,6},{8,9},{9,8},{10,11... | collective-permute-start | bytes 884744 | tf_op jit(solution)/shard_map/ppermute | solution.py:513
  (30 other events, 136.1 us)
where the time goes:
time: 448 us; the launch traced here: 442 us
  Pallas kernels  204 us (46%)
  waiting for transfers between devices  106 us (24%)
  starting transfers between devices  50 us (11%)
  local copies, waits for them, and re-layouts  49.2 us (11%)
  other arithmetic  30.4 us (7%)
    ppermute x58, waiting for transfers between devices, swap_bit(): return lax.ppermute(array, axis, [(i, i ^ 1 << bit) for i in range(size)])  106 us
    pallas_call x1, Pallas kernels, forward(): pl.pallas_call(functools.partial(forward_kernel, (clips, slots, rows)), g...  72.1 us
    pallas_call x3, Pallas kernels, attend_back(): pl.pallas_call(attend_back_kernel, grid=(clips, pairs), in_specs=[tok, ke...  53.8 us
    pallas_call x1, Pallas kernels, mlp(): pl.pallas_call(functools.partial(mlp_kernel, (clips, slots, rows, tile)),...  51.7 us
    ppermute x58, starting transfers between devices, swap_bit(): return lax.ppermute(array, axis, [(i, i ^ 1 << bit) for i in range(size)])  50 us
    convert_element_type x33, other arithmetic, add_low(): return (left.astype(f32) + right.astype(f32)).astype(bf16)  16.9 us
    pallas_call x3, Pallas kernels, weight_grads(): pl.pallas_call(weight_kernel, grid=(3,), in_specs=[full((total, width)),...  16.8 us
    broadcast_in_dim x8, local copies, waits for them, and re-layouts, on_device(): vec = lambda v: v.astype(f32)[None, :]  10.1 us
  transfers between devices with their start and end apart: 58, of which 32 were waited for; matrix products, arithmetic and copies ran while one was open for 13% of the time, Pallas kernels for 18%

commit v1 on v0

--- a/solution.py
+++ b/solution.py
@@ -357,6 +357,407 @@
     )(n2, middle, cot, live, mixed, fc1, b1, fc2, b2, gain, shift, proj)
 
 
+def sum_arrays(width, hidden, clip_size, chunks):
+    rows = width // clip_size
+    tall = hidden // clip_size
+    last = 3 * 2 * chunks
+    first, second = (0, 1, 2), (1, 0, 2)
+    arrays = [
+        ("fc1", 0, rows, hidden // 4, first, (1, 6, 9, 13, 15, 17, last + 2)),
+        ("fc2", 0, tall // 2, width // 2, second, (2, 7, 10, 13, 15, 17, last + 2)),
+        ("fc1", hidden // 4, rows, hidden // 4, first, (3, 11, 14, 17, last, last + 1, last + 2)),
+        ("fc2", tall // 2, tall // 2, width // 2, second, (4, 12, 15, 17, last, last + 1, last + 2)),
+        ("proj", 0, rows, width // 2, second, (5, 12, 15, last, last + 1, last + 2, last + 3)),
+    ]
+    after = [(last + 1, last + 2), (last + 2, last + 3), (last + 3, last + 4)]
+    for chunk in range(chunks):
+        begin = last + chunk + 1
+        stages = tuple(min(begin + i, last + 6) for i in range(7))
+        arrays.append(("qkv", chunk, rows, width // 2, second if chunk == 1 else first, stages))
+    return arrays
+
+
+def backward_kernel(
+    meta,
+    q_ref, k_ref, v_ref, mask_ref, mixed_ref, lse_ref, grad_ref,
+    normed_ref, qkv_ref, tok_ref, gmid_ref, gain_ref, small_ref, db1_ref,
+    dfc1_ref, dfc2_ref, dproj_ref,
+    gtok_ref, fc1_out, fc2_out, proj_out, qkv_out, vec_out,
+    *scratch,
+):
+    clips, slots, rows, bits, pairs, arrays = meta
+    total = clips * rows
+    width = qkv_ref.shape[0]
+    lanes = 2 * DH
+    step = pl.program_id(0)
+    attention = pairs * clips
+    chunks = pairs // 2
+    mesh_id = pl.DeviceIdType.MESH
+    count = len(arrays)
+
+    scratch = list(scratch)
+    take = lambda n: [scratch.pop(0) for _ in range(n)]
+    dq_all, own_kv, far_kv, send_kv, got_kv, across_kv, weights, acc, vec_sum, vec_got = take(10)
+    own_bufs = dict(zip(("fc1", "fc2", "proj"), take(3)))
+    stage_bufs = [take(bits + 1) for _ in arrays]
+    half_bufs = take(count)
+    full_bufs = take(count)
+    kv_send, kv_recv, sum_send, sum_recv, own_sem, vec_send, vec_recv = take(7)
+
+    freq = lax.axis_index("freq")
+    place = lax.axis_index("clip")
+    core = freq % 2
+    vert = freq // 2
+    bit_at = [(place // 2 ** b) % 2 for b in range(bits)]
+    core_dev = {"freq": freq + 1 - 2 * core}
+    vert_dev = {"freq": (freq + 2) % 4}
+    clip_dev = [{"clip": place + (1 - 2 * bit_at[b]) * 2 ** b} for b in range(bits)]
+
+    def remote(src, dst, send, recv, device):
+        return pltpu.make_async_remote_copy(
+            src_ref=src, dst_ref=dst, send_sem=send, recv_sem=recv, device_id=device, device_id_type=mesh_id
+        )
+
+    def kv_core(p):
+        return remote(send_kv.at[p % 2], got_kv.at[p % 2], kv_send.at[0, p], kv_recv.at[0, p], core_dev)
+
+    def kv_vert(p):
+        return remote(far_kv.at[p], across_kv.at[p], kv_send.at[1, p], kv_recv.at[1, p], vert_dev)
+
+    def kv_pass(p):
+        kv_core(p).wait_recv()
+
+        def add_one(i, carry):
+            part, clip = i // clips, i % clips
+            own_kv[p, part, clip] = own_kv[p, part, clip] + got_kv[p % 2, 0, part, clip]
+            far_kv[p, part, clip] = far_kv[p, part, clip] + got_kv[p % 2, 1, part, clip]
+            return carry
+
+        lax.fori_loop(0, 2 * clips, add_one, 0)
+        kv_vert(p).start()
+
+    every = (slice(None),) * bits
+
+    def piece(a, who):
+        name, at, r, width_a, _, _ = arrays[a]
+        if name == "fc1":
+            return dfc1_ref.at[(who,) + every + (slice(None), pl.ds(at, width_a))]
+        if name == "fc2":
+            return dfc2_ref.at[(who,) + every + (pl.ds(at, r), slice(None))]
+        if name == "proj":
+            return dproj_ref.at[who]
+        return weights.at[at, who]
+
+    def chosen(a, stage, index_of):
+        order = arrays[a][4]
+        left = [b for b in range(bits)[::-1] if b not in order[: stage - 1]]
+        bit = order[stage - 1]
+        at = (slice(None),) * left.index(bit) + (index_of(bit),)
+        return stage_bufs[a][stage - 1].at[at]
+
+    def stage_copy(a, stage):
+        half = arrays[a][2] // 2
+        sems = (sum_send.at[a, stage], sum_recv.at[a, stage])
+        if stage == 0:
+            return remote(piece(a, 1 - core), stage_bufs[a][0], *sems, core_dev)
+        if stage <= bits:
+            src = chosen(a, stage, lambda bit: 1 - bit_at[bit])
+            return remote(src, stage_bufs[a][stage], *sems, clip_dev[arrays[a][4][stage - 1]])
+        if stage == bits + 1:
+            src = stage_bufs[a][bits].at[pl.ds((1 - vert) * half, half)]
+            return remote(src, half_bufs[a], *sems, vert_dev)
+        if stage == bits + 2:
+            dst = full_bufs[a].at[core, pl.ds(vert * half, half)]
+            return remote(half_bufs[a], dst, *sems, vert_dev)
+        return remote(full_bufs[a].at[core], full_bufs[a].at[core], *sems, core_dev)
+
+    def own_copy(a):
+        return pltpu.make_async_copy(piece(a, core), own_bufs[arrays[a][0]], own_sem.at[a])
+
+    def add_blocks(dst, src, lead):
+        if lead == 0:
+            dst[...] = dst[...] + src[...]
+            return
+
+        def add_one(i, carry):
+            at = tuple((i // 2 ** (lead - 1 - j)) % 2 for j in range(lead))
+            dst[at] = dst[at] + src[at]
+            return carry
+
+        lax.fori_loop(0, 2 ** lead, add_one, 0)
+
+    def stage_end(a, stage):
+        name, at, r, _, _, _ = arrays[a]
+        stage_copy(a, stage).wait_recv()
+        if stage == 0:
+            if name == "qkv":
+                add_blocks(stage_bufs[a][0], weights.at[at, core], bits)
+            else:
+                own_copy(a).wait()
+                add_blocks(stage_bufs[a][0], own_bufs[name], bits)
+                again = [b for b in range(a + 1, count) if arrays[b][0] == name]
+                if again:
+                    own_copy(again[0]).start()
+        elif stage <= bits:
+            add_blocks(stage_bufs[a][stage], chosen(a, stage, lambda bit: bit_at[bit]), bits - stage)
+        elif stage == bits + 1:
+            half = r // 2
+            mine = pl.ds(pl.multiple_of(vert * half, half), half)
+            value = half_bufs[a][...] + stage_bufs[a][bits][mine]
+            half_bufs[a][...] = value
+            full_bufs[a][core, mine] = value
+        if stage == 0 and a in (2, 3):
+            return
+        if stage == 1 and a in (0, 1):
+            stage_copy(a + 2, 1).start()
+        if stage < bits + 3:
+            stage_copy(a, stage + 1).start()
+
+    def vec_copy(hop):
+        device = core_dev if hop == 0 else vert_dev if hop == 1 else clip_dev[hop - 2]
+        return remote(vec_sum.at[hop], vec_got.at[hop], vec_send.at[hop], vec_recv.at[hop], device)
+
+    def vec_end(hop):
+        vec_copy(hop).wait_recv()
+        vec_sum[hop + 1] = vec_sum[hop] + vec_got[hop]
+        if hop < bits + 1:
+            vec_copy(hop + 1).start()
+
+    final = attention + chunks + clips
+    events = {}
+    for a, entry in enumerate(arrays):
+        for stage, at in enumerate(entry[5]):
+            events.setdefault(at, []).append(functools.partial(stage_end, a, stage))
+    for p in range(pairs):
+        events.setdefault(clips * p + clips + 1, []).append(functools.partial(kv_pass, p))
+        if p >= 2:
+            events.setdefault(clips * p, []).append(lambda p=p: kv_core(p - 2).wait_send())
+
+    @pl.when(step == 0)
+    def enter():
+        barrier = pltpu.get_barrier_semaphore()
+        for device in [core_dev, vert_dev] + clip_dev:
+            pl.semaphore_signal(barrier, inc=1, device_id=device, device_id_type=mesh_id)
+        pl.semaphore_wait(barrier, 2 + bits)
+        for a in (0, 1, 2, 3, 4):
+            stage_copy(a, 0).start()
+        for a in (0, 1, 4):
+            own_copy(a).start()
+        vec_sum[0] = jnp.zeros_like(vec_sum[0])
+        vec_sum[0, 4:8] = small_ref[0:4]
+        for i in range(db1_ref.shape[1] // width):
+            vec_sum[0, 8 + i : 9 + i] = db1_ref[0:1, i * width : (i + 1) * width]
+        acc[...] = jnp.zeros_like(acc)
+
+    for at in sorted(events):
+        if at < final:
+            @pl.when(step == at)
+            def run(at=at):
+                for action in events[at]:
+                    action()
+
+    @pl.when(step < attention)
+    def attend():
+        p = step // clips
+        clip = step % clips
+        query = q_ref[0]
+        keys = k_ref[0]
+        values = v_ref[0]
+        grad = grad_ref[0]
+        live = mask_ref[0] > 0.5
+        product = grad.astype(f32) * mixed_ref[0].astype(f32)
+        dqs, dk, dv = [], None, None
+        for head in range(2):
+            own_query = only(query, head)
+            own_grad = only(grad, head)
+            scores = jnp.where(live, dot(own_query, keys, NT), MASKED)
+            probs = jnp.exp(scores - lse_ref[0, :, head * DH : head * DH + 1])
+            delta = jnp.sum(only(product, head), axis=1, keepdims=True)
+            dscores = (probs * (dot(own_grad, values, NT) - delta)).astype(bf16)
+            dqs.append(dot(dscores, keys))
+            more_k = dot(dscores, own_query, TN)
+            more_v = dot(probs.astype(bf16), own_grad, TN)
+            dk = more_k if dk is None else dk + more_k
+            dv = more_v if dv is None else dv + more_v
+        first = own_lanes(dqs[0].shape, 0)
+        dq = (jnp.where(first, dqs[0], dqs[1]) * DH ** -0.5).astype(bf16)
+        dq_all[p, pl.ds(pl.multiple_of(clip * rows, rows), rows)] = dq
+        for part, value in enumerate((dk, dv)):
+            low = value.astype(bf16)
+            own_kv[p, part, clip] = low[:rows]
+            far_kv[p, part, clip] = low[rows : 2 * rows]
+            send_kv[p % 2, 0, part, clip] = low[2 * rows : 3 * rows]
+            send_kv[p % 2, 1, part, clip] = low[3 * rows :]
+
+    for p in range(pairs):
+        @pl.when(step == clips * p + clips - 1)
+        def send_pair(p=p):
+            kv_core(p).start()
+
+    for j in range(chunks):
+        @pl.when(step == attention + j)
+        def weights_of(j=j):
+            columns = []
+            for p in (2 * j, 2 * j + 1):
+                kv_vert(p).wait_recv()
+                at = slice(p * lanes, (p + 1) * lanes)
+                query = dq_all[p]
+                key, value = [
+                    (own_kv[p, part] + across_kv[p, part]).reshape(total, lanes) for part in range(2)
+                ]
+                vec_sum[0, 2:3, at] = column_sums(query.astype(f32))
+                vec_sum[0, 3:4, at] = column_sums(value.astype(f32))
+                columns += [query, key, value]
+            wide = jnp.concatenate(columns, axis=1)
+            grads = dot(normed_ref[...], wide, TN).astype(bf16)
+            shape = weights.shape[2:]
+            for half in range(2):
+                weights[j, half] = grads[:, half * 3 * lanes : (half + 1) * 3 * lanes].reshape(shape)
+            stage_copy(5 + j, 0).start()
+            for part in range(3):
+                low = jnp.concatenate([columns[part], columns[3 + part]], axis=1)
+                at = part * width + 2 * j * lanes
+                acc[...] += dot(low, qkv_ref[:, at : at + 2 * lanes], NT)
+
+    @pl.when((step >= attention + chunks) & (step < final))
+    def inputs():
+        clip = step - (attention + chunks)
+        at = pl.ds(pl.multiple_of(clip * rows, rows), rows)
+        grad = acc[at]
+        unit, inverse = center_scale(tok_ref[0].astype(f32))
+        result = gmid_ref[0] + norm_back(unit, inverse, gain_ref[...], grad)
+        gtok_ref[0] = result[:slots]
+        vec_sum[0, 0:1] += column_sums(grad * unit)
+        vec_sum[0, 1:2] += column_sums(grad)
+
+    @pl.when(step == final)
+    def finish():
+        vec_copy(0).start()
+        rest = [action for at in sorted(events) if at >= final for action in events[at]]
+        hops = [functools.partial(vec_end, hop) for hop in range(bits + 2)]
+        while rest or hops:
+            if hops:
+                hops.pop(0)()
+            if rest:
+                rest.pop(0)()
+        for a, (name, at, r, width_a, _, _) in enumerate(arrays):
+            for who in range(2):
+                value = full_bufs[a][who]
+                if name == "fc1":
+                    start = who * fc1_out.shape[1] // 2 + at
+                    fc1_out[:, start : start + width_a] = value
+                elif name == "fc2":
+                    fc2_out[at : at + r, who * width_a : (who + 1) * width_a] = value
+                elif name == "proj":
+                    proj_out[:, who * width_a : (who + 1) * width_a] = value
+                else:
+                    for part in range(3):
+                        start = part * width + (2 * at + who) * lanes
+                        qkv_out[:, start : start + lanes] = value[:, part * lanes : (part + 1) * lanes]
+        vec_out[...] = vec_sum[bits + 2]
+        for a in range(count):
+            for stage in range(bits + 4):
+                stage_copy(a, stage).wait_send()
+        for p in range(pairs):
+            if p >= pairs - 2:
+                kv_core(p).wait_send()
+            kv_vert(p).wait_send()
+        for hop in range(bits + 2):
+            vec_copy(hop).wait_send()
+
+
+def backward(q, k, v, mask, mixed, lse, gmixed, normed, qkv_weight, tok, gmid, gain, small, db1,
+             dfc1, dfc2, dproj, slots, clip_size):
+    clips, rows, width = q.shape
+    keys = k.shape[1]
+    total = clips * rows
+    pairs = HEADS // 2
+    lanes = 2 * DH
+    chunks = pairs // 2
+    bits = clip_size.bit_length() - 1
+    hidden = db1.shape[1]
+    arrays = sum_arrays(width, hidden, clip_size, chunks)
+    attention = pairs * clips
+    steps = attention + chunks + clips + 1
+    one = pl.Buffered(buffer_count=1)
+
+    def of_pair(s):
+        at = jnp.minimum(s, attention - 1)
+        return at % clips, 0, at // clips
+
+    def of_clip(s):
+        return jnp.clip(s - attention - chunks, 0, clips - 1), 0, 0
+
+    fixed = lambda shape: pl.BlockSpec(shape, lambda s: (0,) * len(shape), pipeline_mode=one)
+    tok_pair = pl.BlockSpec((1, rows, lanes), of_pair)
+    key_pair = pl.BlockSpec((1, keys, lanes), of_pair)
+    tok_clip = pl.BlockSpec((1, rows, width), of_clip)
+    anywhere = pl.BlockSpec(memory_space=pl.ANY)
+    blocks = (2,) * bits
+    r_fc1, r_fc2 = width // clip_size, hidden // clip_size
+    dfc1 = dfc1.reshape((2,) + blocks + (r_fc1, hidden // 2))
+    dfc2 = dfc2.reshape((2,) + blocks + (r_fc2, width // 2))
+    dproj = dproj.reshape((2,) + blocks + (r_fc1, width // 2))
+    vmem = lambda *shape: pltpu.VMEM(shape, bf16)
+    scratch = [
+        vmem(pairs, total, lanes),
+        vmem(pairs, 2, clips, rows, lanes),
+        vmem(pairs, 2, clips, rows, lanes),
+        vmem(2, 2, 2, clips, rows, lanes),
+        vmem(2, 2, 2, clips, rows, lanes),
+        vmem(pairs, 2, clips, rows, lanes),
+        vmem(chunks, 2, *blocks, r_fc1, 3 * lanes),
+        pltpu.VMEM((total, width), f32),
+        pltpu.VMEM((bits + 3, 16, width), f32),
+        pltpu.VMEM((bits + 2, 16, width), f32),
+        vmem(*blocks, r_fc1, hidden // 4),
+        vmem(*blocks, r_fc2 // 2, width // 2),
+        vmem(*blocks, r_fc1, width // 2),
+    ]
+    for _, _, r, width_a, _, _ in arrays:
+        scratch += [vmem(*((2,) * (bits - stage)), r, width_a) for stage in range(bits + 1)]
+    scratch += [vmem(r // 2, width_a) for _, _, r, width_a, _, _ in arrays]
+    scratch += [vmem(2, r, width_a) for _, _, r, width_a, _, _ in arrays]
+    dma = lambda *shape: pltpu.SemaphoreType.DMA(shape)
+    scratch += [
+        dma(2, pairs), dma(2, pairs), dma(len(arrays), bits + 4), dma(len(arrays), bits + 4),
+        dma(len(arrays)), dma(bits + 2), dma(bits + 2),
+    ]
+    return pl.pallas_call(
+        functools.partial(backward_kernel, (clips, slots, rows, bits, pairs, arrays)),
+        grid=(steps,),
+        in_specs=[
+            tok_pair, key_pair, key_pair,
+            pl.BlockSpec((1, 1, keys), lambda s: (of_pair(s)[0], 0, 0)),
+            tok_pair, tok_pair, tok_pair,
+            fixed((total, width)), fixed(qkv_weight.shape), tok_clip, tok_clip,
+            fixed((1, width)), fixed((8, width)), fixed((1, hidden)),
+            anywhere, anywhere, anywhere,
+        ],
+        out_specs=[
+            pl.BlockSpec((1, slots, width), of_clip),
+            fixed((r_fc1, hidden)), fixed((r_fc2, width)), fixed((r_fc1, width)),
+            fixed((r_fc1, 3 * width)), fixed((16, width)),
+        ],
+        out_shape=[
+            jax.ShapeDtypeStruct((clips, slots, width), f32),
+            jax.ShapeDtypeStruct((r_fc1, hidden), bf16),
+            jax.ShapeDtypeStruct((r_fc2, width), bf16),
+            jax.ShapeDtypeStruct((r_fc1, width), bf16),
+            jax.ShapeDtypeStruct((r_fc1, 3 * width), bf16),
+            jax.ShapeDtypeStruct((16, width), f32),
+        ],
+        scratch_shapes=scratch,
+        compiler_params=params(collective_id=1, has_side_effects=True),
+        cost_estimate=pl.CostEstimate(
+            flops=2 * total * (5 * keys * width + 6 * width * width),
+            bytes_accessed=60_000_000,
+            transcendentals=total * keys * HEADS,
+        ),
+        name="backward",
+    )(q, k, v, mask, mixed, lse, gmixed, normed, qkv_weight, tok, gmid, gain, small, db1, dfc1, dfc2, dproj)
+
+
 def attend_back_kernel(q_ref, k_ref, v_ref, mask_ref, mixed_ref, lse_ref, grad_ref,
                        dq_ref, dkeep_ref, dsend_ref):
     query = q_ref[0]
@@ -583,7 +984,10 @@
     tok = jnp.concatenate(
         [tokens, jnp.broadcast_to(kept[:, :, None], (clips, rows - slots, width))], axis=1
     )
-    vectors = [vec(v) for v in (query_bias, value_bias, attn_gain, attn_shift, proj_bias, mlp_gain, mlp_shift)]
+    stacked = jnp.stack(
+        [query_bias, value_bias, attn_gain, attn_shift, proj_bias, mlp_gain, mlp_shift, fc2_bias]
+    ).astype(f32)
+    vectors = [stacked[i : i + 1] for i in range(7)]
     q, k, v, normed, mixed, lse, middle, normed2, mask = forward(
         tok, slots, qkv_weight, vectors, proj_weight
     )
@@ -593,6 +997,16 @@
         flat(normed2), flat(middle), flat(cot), live, flat(mixed), fc1_weight, vec(fc1_bias),
         fc2_weight, vec(fc2_bias), vectors[5], vectors[6], proj_weight, (clips, slots, rows),
     )
+    if clip_size == 8 and width % (32 * clip_size) == 0:
+        grad_tokens, low_fc1, low_fc2, low_proj, low_qkv, summed = backward(
+            q, k, v, mask, mixed, lse, gmixed.reshape(clips, rows, width), flat(normed), qkv_weight, tok,
+            gmid.reshape(clips, rows, width), vectors[2], small2, db1, dfc1, dfc2, dproj, slots, clip_size,
+        )
+        return (
+            layer_out, grad_tokens, summed[0], summed[1], low_qkv.astype(f32), summed[2], summed[3],
+            low_proj.astype(f32), summed[7], summed[4], summed[5], low_fc1.astype(f32),
+            summed[8:12].reshape(-1), low_fc2.astype(f32), summed[6],
+        )
     early = total_sum(jnp.concatenate([small2[:4].reshape(-1), db1.reshape(-1)])[None, :], clip_size)[0]
     sum_fc1 = gather_low(scatter_sum(dfc1, clip_size, forward_order))
     sum_fc2 = gather_low(scatter_sum(dfc2, clip_size, second_order))

time: 448 us -> 308 us (0.69); the launches traced: 442 us -> 306 us
  waiting for transfers between devices: 106 us -> 0 us
  Pallas kernels: 204 us -> 280 us
  starting transfers between devices: 50 us -> 0 us
  local copies, waits for them, and re-layouts: 49.2 us -> 13.4 us
  other arithmetic: 30.4 us -> 12.5 us
    ppermute x58 -> x0, waiting for transfers between devices: 106 us -> none  [swap_bit(): return lax.ppermute(array, axis, [(i, i ^ 1 << bit) for i in range(size)])]
    pallas_call x7 -> x1, Pallas kernels: 80 us -> 156 us  [backward(): pl.pallas_call(functools.partial(backward_kernel, (clips, slots, rows, bi...]
    ppermute x58 -> x0, starting transfers between devices: 50 us -> none  [swap_bit(): return lax.ppermute(array, axis, [(i, i ^ 1 << bit) for i in range(size)])]
    convert_element_type x36 -> x4, other arithmetic: 20 us -> 5.89 us  [the longest x1 2.04 us: on_device(): low_qkv.astype(f32)]
    squeeze x25 -> x0, local copies, waits for them, and re-layouts: 12.4 us -> none  [the longest x21 7.09 us: pick(): return lax.dynamic_index_in_dim(array, index, dim, keepdims=False)]
    slice x11 -> x3, local copies, waits for them, and re-layouts: 13.8 us -> 3.33 us  [the longest x1 1.92 us: on_device(): summed[6]]
    broadcast_in_dim x8 -> x0, local copies, waits for them, and re-layouts: 10.1 us -> none  [on_device(): vec = lambda v: v.astype(f32)[None, :]]
    another operation x0 -> x9, local copies, waits for them, and re-layouts: none -> 5.53 us  [on_device(): jnp.stack([query_bias, value_bias, attn_gain, attn_shift, proj_bias, mlp_...]
  transfers between devices with their start and end apart: 58 -> 0, of which waited for: 32 -> 0; matrix products, arithmetic and copies ran while one was open for 13% -> 0% of each run, Pallas kernels for 18% -> 0%
where the time goes in v1:
time: 308 us; the launch traced here: 306 us
  Pallas kernels  280 us (91%)
  local copies, waits for them, and re-layouts  13.4 us (4%)
  other arithmetic  12.5 us (4%)
    pallas_call x1, Pallas kernels, backward(): pl.pallas_call(functools.partial(backward_kernel, (clips, slots, rows, bi...  156 us
    pallas_call x1, Pallas kernels, forward(): pl.pallas_call(functools.partial(forward_kernel, (clips, slots, rows)), g...  71.9 us
    pallas_call x1, Pallas kernels, mlp(): pl.pallas_call(functools.partial(mlp_kernel, (clips, slots, rows, tile)),...  51.4 us

profile of v1, /device:TPU:0, one launch (start us, length us, event | category | flops | bytes accessed | tf_op | source)
XLA Modules:
  0.0 306.2 jit_solution(12991599826344134861)
XLA Ops:
  0.6 0.7 convert_bitcast_fusion
  1.3 0.7 stack.29
  2.0 0.7 stack.30
  2.7 0.7 stack.27
  3.4 0.7 stack.28
  4.0 0.7 stack.31
  4.7 0.7 stack.32
  5.4 0.7 stack.33
  6.1 1.3 reshape_convert_fusion.b2_ref
  7.4 0.7 stack.34
  8.1 0.7 fusion
  8.8 0.6 fusion.1
  9.4 1.3 broadcast_in_dim.22
  10.7 0.1 broadcast_in_dim.18
  10.8 1.0 reshape.105.live_ref
  11.8 0.0 copy-start.1
  11.8 2.6 pad_maximum_fusion.tok_ref
  14.5 0.0 copy-done.1
  14.5 1.2 pad.4
  15.7 71.9 %forward.1 = (bf16[3,304,768]{2,1,0:T(8,128)(2,1)}, bf16[3,1216,768]{2,1,0:T(8,128)(2,1)}, bf16[3,1216,768]{2,1,0:T(8,128)(2,1)}, bf16[3,304,768]{2,1,0:T(8,128)...) custom-call(bf16[3,304,768]{2,1,0:T(8,128)(2,1)} %pad_maximum_fusion, ...), custom_call_target="tpu_custom_call" | custom-call | flops 14165213184 | bytes 40000000 | tf_op jit(solution)/shard_map/forward/pallas_call | solution.py:185
  87.6 51.4 %mlp.1 = (bf16[3,298,768]{2,1,0:T(8,128)(2,1)}, bf16[2,768,1536]{2,1,0:T(8,128)(2,1)}, bf16[2,3072,384]{2,1,0:T(8,128)(2,1)}, bf16[2,768,384]{2,1,0:T(8,128)(2,1...) custom-call(bf16[912,768]{1,0:T(8,128)(2,1)} %bitcast.24, ...), custom_call_target="tpu_custom_call" | custom-call | flops 25820135424 | bytes 40000000 | tf_op jit(solution)/shard_map/mlp/pallas_call | solution.py:309
  139.0 156.3 %backward.1 = (f32[3,298,768]{2,1,0:T(8,128)}, bf16[96,3072]{1,0:T(8,128)(2,1)}, bf16[384,768]{1,0:T(8,128)(2,1)}, bf16[96,768]{1,0:T(8,128)(2,1)}, bf16[96,2304]{1,0:T(8,128)(2,1)}, /*index=5*/f32[16,768]{1,0:T(8,128)}) custom-call(bf16[3,304,768]{2,1,0:T(8,128)(2,1)} %get-tuple-element.42.q_ref, bf16[3,1216,768]{2,1,0:T(8,128)(2,1)} %get-tuple-element.43.k_ref, ...), custom_call_target="tpu_custom_call" | custom-call | flops 14972092416 | bytes 60000000 | tf_op jit(solution)/shard_map/backward/pallas_call | solution.py:726
  295.3 0.0 copy-start.3
  295.3 0.8 slice.62
  296.1 1.9 slice_reduce_fusion
  298.0 0.6 reshape.102
  298.6 1.6 convert_element_type.40
  300.2 0.0 copy-start.2
  300.2 2.0 convert_element_type.39
  302.3 0.0 copy-done.3
  302.3 0.0 copy-start
  302.3 1.1 convert_element_type.41
  303.4 0.0 copy-done.2
  303.4 1.1 convert_element_type.42
  304.5 0.1 copy-done
  304.7 1.6 copy.33
  (1 shorter events, 0.0 us)
Async XLA Ops:
  11.8 2.7 copy-start.1
  295.3 7.0 %copy-start.3 = (bf16[96,3072]{1,0:T(8,128)(2,1)S(1)}, bf16[96,3072]{1,0:T(8,128)(2,1)}, u32[]{:S(2)}) copy-start(bf16[96,3072]{1,0:T(8,128)(2,1)} %get-tuple-element.59) | copy-start | bytes 1769476
  300.2 3.2 %copy-start.2 = (bf16[384,768]{1,0:T(8,128)(2,1)S(1)}, bf16[384,768]{1,0:T(8,128)(2,1)}, u32[]{:S(2)}) copy-start(bf16[384,768]{1,0:T(8,128)(2,1)} %get-tuple-element.60) | copy-start | bytes 1769476
  302.3 2.4 copy-start
